TPU v7x, 256 devices: a whole 4x4x8 slice. The times are simulated.
256 devices in a mesh: coarse: 8 (over z_hi, x), fine: 8 (over y, core), swath: 4 (over z_lo).
Axes of the slice: x: 4, y: 4, z: 8 (z_hi: 2, z_lo: 4; z = z_hi * 4 + z_lo), core: 2. Of those that a mesh axis runs over, the one named last changes fastest.
Arguments:
- echoes: int32 [256, 64, 2, 2048], P(('coarse', 'fine'), None, None, 'swath'), may hold values from -127 to 127
- exponents: int32 [256, 64, 64], P(('coarse', 'fine'), None, 'swath'), may hold values from 0 to 3
- replica: bfloat16 [2, 129], replicated, may hold values from -0.375 to 0.375
- interp0: bfloat16 [2, 256, 64, 64], P(None, ('coarse', 'fine')), may hold values from -0.5 to 0.5
- upsample1: bfloat16 [2, 256, 64, 512], P(None, ('coarse', 'fine')), may hold values from -0.125 to 0.125
- phase1: bfloat16 [512, 256, 2048], P(None, ('coarse', 'fine'), 'swath'), may hold values from -3.140625 to 3.140625
- upsample2: bfloat16 [16, 2, 512, 2048], P('coarse', None, 'fine'), may hold values from -0.046875 to 0.046875
- phase2: bfloat16 [2048, 16, 2048], P(None, 'coarse', 'swath'), may hold values from -3.140625 to 3.140625
Outputs:
- image: float32 [2048, 2, 2048], P(('coarse', 'fine'), None, 'swath')
All inputs are finite; a program needn't handle non-finite values.
Results may differ from a plain program's by a relative error of at most 0.005.
Values may be sent and summed in bfloat16 or wider, within the bound.
No kernel may reach another device: no remote copies, remote signals or barrier semaphores. Data moves between devices by JAX's collectives and lax.ppermute only.
A program may use at most 128 MiB of HBM per device.

v0:
```python
import jax
import jax.numpy as jnp
from jax import lax
from jax.experimental import pallas as pl
from jax.experimental.pallas import tpu as pltpu
from jax.sharding import PartitionSpec as P


F32 = jnp.float32
BF16 = jnp.bfloat16

SIN = (0.7071067690849304, -0.029462749138474464, 0.0003682656097225845, -2.1877108338230755e-06, 7.155278591852721e-09)
COS = (1.4142135381698608, -0.17677636444568634, 0.003682575421407819, -3.061265670112334e-05, 1.279087769034959e-07)
VMEM = pltpu.MemorySpace.VMEM
PARAMS = pltpu.CompilerParams(vmem_limit_bytes=16 << 20)
WHOLE = pl.BlockSpec(memory_space=pltpu.MemorySpace.VMEM)


def horner(u, coefs):
    total = coefs[-1] * u + coefs[-2]
    for c in coefs[-3::-1]:
        total = total * u + c
    return total


def cos_sin(x):
    u = x * x
    s = x * horner(u, SIN)
    return 1.0 - s * s, s * horner(u, COS)


def near(x):
    return pltpu.with_memory_space_constraint(x, VMEM)


def swap_cores(x):
    return lax.ppermute(x, "fine", [(i, i ^ 1) for i in range(8)])


def shift_chips(x, d):
    return lax.ppermute(x, "fine", [(y * 2 + k, (y + d) % 4 * 2 + k) for y in range(4) for k in range(2)])


def shift_x(x, d):
    return lax.ppermute(x, "coarse", [(z * 4 + i, z * 4 + (i + d) % 4) for z in range(2) for i in range(4)])


def swap_z(x):
    return lax.ppermute(x, "coarse", [(i, i ^ 4) for i in range(8)])


def pick(x, i, axis=0):
    return lax.dynamic_index_in_dim(x, i, axis, keepdims=False)


def tdot(a, b):
    return lax.dot_general(a, b, (((0,), (0,)), ((), ())), preferred_element_type=F32)


def factors(expo, lo, lanes):
    blocks = expo.shape[0]
    bins = lo + lax.broadcasted_iota(jnp.int32, (blocks, lanes), 1)
    expand = bins // 32 == lax.broadcasted_iota(jnp.int32, (blocks, lanes), 0)
    scale = (jnp.left_shift(1, expo).astype(F32) * (1.0 / 256.0)).astype(BF16)
    return tdot(scale, expand.astype(F32).astype(BF16))


def ends_kernel(low_ref, high_ref, expo_ref, even_ref, odd_ref):
    odd = (lax.axis_index("swath") & 1) == 1
    subs, pings, _, lanes = low_ref.shape
    low = lax.broadcasted_iota(jnp.int32, (pings, lanes), 1) < 64
    start = 32 * expo_ref.shape[1] - lanes
    for s in range(subs):
        factor = factors(expo_ref[s], 0, lanes)
        re = low_ref[s, :, 0, :].astype(F32) * factor
        im = low_ref[s, :, 1, :].astype(F32) * factor
        first = jnp.where(low, re, pltpu.roll(im, 64, 1))
        factor = factors(expo_ref[s], start, lanes)
        re = high_ref[s, :, 0, :].astype(F32) * factor
        im = high_ref[s, :, 1, :].astype(F32) * factor
        last = jnp.where(low, pltpu.roll(re, 64, 1), im)
        even_ref[s] = jnp.where(odd, first, last).astype(BF16)
        odd_ref[s] = jnp.where(odd, last, first).astype(BF16)


def ends(echoes, exponents):
    s, l, _, r = echoes.shape
    b = exponents.shape[1]
    shape = jax.ShapeDtypeStruct((s, l, 128), BF16)
    whole = pl.BlockSpec((s, l, 128), lambda i: (0, 0, 0))
    return pl.pallas_call(
        ends_kernel,
        grid=(1,),
        in_specs=[
            pl.BlockSpec((s, l, 2, 128), lambda i: (0, 0, 0, 0)),
            pl.BlockSpec((s, l, 2, 128), lambda i: (0, 0, 0, r // 128 - 1)),
            pl.BlockSpec((s, b, l), lambda i: (0, 0, 0)),
        ],
        out_specs=[whole, whole],
        out_shape=[shape, shape],
        name="ends",
        compiler_params=PARAMS,
    )(echoes, echoes, exponents)


def prep_kernel(echo_ref, expo_ref, out_ref):
    for s in range(echo_ref.shape[0]):
        factor = factors(expo_ref[s], 0, echo_ref.shape[3])
        for i in (0, 1):
            out_ref[s, i] = (echo_ref[s, :, i, :].astype(F32) * factor).astype(BF16)


def prep(echoes, exponents):
    s, l, _, r = echoes.shape
    b = exponents.shape[1]
    return pl.pallas_call(
        prep_kernel,
        grid=(2,),
        in_specs=[
            pl.BlockSpec((s // 2, l, 2, r), lambda i: (i, 0, 0, 0)),
            pl.BlockSpec((s // 2, b, l), lambda i: (i, 0, 0)),
        ],
        out_specs=pl.BlockSpec((s // 2, 2, l, r), lambda i: (i, 0, 0, 0)),
        out_shape=jax.ShapeDtypeStruct((s, 2, l, r), BF16),
        name="prep",
        compiler_params=PARAMS,
    )(echoes, exponents)


def core():
    return lax.axis_index("fine") & 1


def pack_kernel(own_ref, other_ref, *out_refs):
    fine = lax.axis_index("fine")
    k = fine & 1
    rows = own_ref.shape[2]
    low = lax.broadcasted_iota(jnp.int32, (rows, 128), 1) < 64
    for d, out in enumerate(out_refs):
        y = ((fine >> 1) + d) & 3
        even = (y & 1) == 0
        base = pl.multiple_of((y >> 1) * 128, 128)
        for ref, half in ((own_ref, k), (other_ref, 1 - k)):
            at = pl.ds(pl.multiple_of(half * rows, rows), rows)
            for p in range(4):
                a = ref[0, 0, :, pl.ds(base + p * 512, 128)].astype(F32)
                b = ref[0, 0, :, pl.ds(base + p * 512 + 256, 128)].astype(F32)
                c = pltpu.roll(jnp.where(even, b, a), 64, 1)
                out[0, at, p * 128 : (p + 1) * 128] = jnp.where(low, jnp.where(even, a, c), jnp.where(even, c, b)).astype(BF16)


def pack(own, other):
    _, i, rows, m = own.shape
    shape = jax.ShapeDtypeStruct((2, 2 * rows, m // 4), BF16)
    window = pl.BlockSpec((1, 1, rows, m), lambda g: (core(), g, 0, 0))
    return pl.pallas_call(
        pack_kernel,
        grid=(i,),
        in_specs=[window, window],
        out_specs=[pl.BlockSpec((1,) + shape.shape[1:], lambda g: (g, 0, 0))] * 4,
        out_shape=[shape] * 4,
        name="pack",
        compiler_params=PARAMS,
    )(own, other)


def weights_kernel(u_own, u_other, ph_other, mix_ref, ph_ref):
    kid = pl.program_id(0)
    kids = pl.num_programs(0)
    for i, u in enumerate((u_own, u_other)):
        ur = u[0, 0]
        ui = u[1, 0]
        mix_ref[i * kids + kid, 0] = jnp.concatenate([ur, -ui], axis=0).T
        mix_ref[i * kids + kid, 1] = jnp.concatenate([ui, ur], axis=0).T
    ph_ref[kid] = ph_other[0]


def weights(u_own, u_other, ph_other):
    i, s, b, n = u_own.shape
    _, _, r = ph_other.shape
    kids = s // 2
    window = pl.BlockSpec((i, 1, b, n), lambda g: (0, core() * kids + g, 0, 0))
    return pl.pallas_call(
        weights_kernel,
        grid=(kids,),
        in_specs=[window, window, pl.BlockSpec((1, n, r), lambda g: (core() * kids + g, 0, 0))],
        out_specs=[WHOLE, WHOLE],
        out_shape=[pltpu.VMEM((s, 2, n, 2 * b), BF16), pltpu.VMEM((kids, n, r), BF16)],
        name="weights",
        compiler_params=PARAMS,
    )(u_own, u_other, ph_other)


def band_kernel(line_ref, band_ref):
    def band(row):
        full = jnp.broadcast_to(line_ref[row : row + 1, :], (384, 512))
        return pltpu.roll(full, 448, 1, stride=1, stride_axis=0)[:, :128]

    hr = band(0)
    hi = band(1)
    band_ref[0] = jnp.concatenate([hr, -hi], axis=1).astype(BF16)
    band_ref[1] = jnp.concatenate([hi, hr], axis=1).astype(BF16)


def bands(replica):
    taps = replica.astype(F32)
    line = jnp.concatenate([taps[:, :1], jnp.zeros((2, 383), F32), taps[:, :0:-1]], axis=1)
    return pl.pallas_call(band_kernel, out_shape=jax.ShapeDtypeStruct((2, 384, 256), BF16), name="bands", compiler_params=PARAMS)(line)


def beams_kernel(x_ref, even_ref, odd_ref, band_ref, w_ref, out_ref):
    swath = lax.axis_index("swath")
    odd = (swath & 1) == 1
    even_end = even_ref[...].astype(F32)
    odd_end = odd_ref[...].astype(F32)
    left = jnp.where(swath == 0, 0.0, jnp.where(odd, even_end, odd_end)).astype(BF16)
    right = jnp.where(swath == lax.axis_size("swath") - 1, 0.0, jnp.where(odd, odd_end, even_end)).astype(BF16)
    subs, _, pings, bins = x_ref.shape
    rows = subs * pings
    tiles = bins // 128

    def tile(ri, j):
        return x_ref[:, ri, :, j * 128 : (j + 1) * 128].reshape(rows, 128)

    cre = []
    cim = []
    for j in range(tiles):
        near = [t for t in (j - 1, j, j + 1) if 0 <= t < tiles]
        lhs = [tile(ri, t) for ri in (0, 1) for t in near]
        lo = 128 * (near[0] - j + 1)
        hi = 128 * (near[-1] - j + 2)
        rhs = [band_ref[0, lo:hi], band_ref[1, lo:hi]]
        if j == 0:
            lhs.append(left.reshape(rows, 128))
            rhs += [band_ref[0, 64:128], band_ref[1, 64:128]]
        if j == tiles - 1:
            lhs.append(right.reshape(rows, 128))
            rhs += [band_ref[0, 256:320], band_ref[1, 256:320]]
        c = jnp.dot(jnp.concatenate(lhs, axis=1), jnp.concatenate(rhs, axis=0), preferred_element_type=F32)
        cre.append(c[:, :128].astype(BF16))
        cim.append(c[:, 128:].astype(BF16))
    for s in range(subs):
        part = slice(s * pings, (s + 1) * pings)
        c = jnp.concatenate([jnp.concatenate([t[part] for t in cre], axis=1), jnp.concatenate([t[part] for t in cim], axis=1)], axis=0)
        wr = w_ref[0, s]
        wi = w_ref[1, s]
        out_ref[s, 0] = tdot(jnp.concatenate([wr, -wi], axis=0), c).astype(BF16)
        out_ref[s, 1] = tdot(jnp.concatenate([wi, wr], axis=0), c).astype(BF16)


def beams_of(samples, left, right, band, interp0):
    s, _, _, r = samples.shape
    b = interp0.shape[3]
    return pl.pallas_call(beams_kernel, out_shape=pltpu.VMEM((s, 2, b, r), BF16), name="beams", compiler_params=PARAMS)(
        samples, left, right, band, interp0
    )


def level_kernel(d, mix_ref, ph_own, ph_other, b_own, b_other, out_ref, turn_ref):
    fine = lax.axis_index("fine")
    k = fine & 1
    kids = ph_other.shape[0]
    n = out_ref.shape[1]
    base = pl.multiple_of((((fine >> 1) + d) & 3) * n, n)
    rows = pl.ds(base, n)
    for i, b in enumerate((b_own, b_other)):
        for s in range(kids):
            rhs = b[k * kids + s].reshape(-1, b.shape[3])
            for c in (0, 1):
                turn_ref[i * kids + s, c] = jnp.dot(mix_ref[i * kids + s, c, rows, :], rhs, preferred_element_type=F32)

    step = 16

    def body(j, carry):
        at = pl.ds(pl.multiple_of(j * step, step), step)
        there = pl.ds(pl.multiple_of(base + j * step, step), step)
        re = im = None
        for i, (ph, first) in enumerate(((ph_own, k * kids), (ph_other, 0))):
            for s in range(kids):
                c, t = cos_sin(ph[first + s, there, :].astype(F32))
                tr = turn_ref[i * kids + s, 0, at, :]
                ti = turn_ref[i * kids + s, 1, at, :]
                pr = c * tr - t * ti
                pi = t * tr + c * ti
                re = pr if re is None else re + pr
                im = pi if im is None else im + pi
        out_ref[0, at, :] = re.astype(out_ref.dtype)
        out_ref[1, at, :] = im.astype(out_ref.dtype)
        return carry

    lax.fori_loop(0, n // step, body, 0)


def level_part(d, dtype, *operands):
    mix, ph = operands[:2]
    s, _, n, _ = mix.shape
    n //= 4
    r = ph.shape[2]
    return pl.pallas_call(
        lambda *refs: level_kernel(d, *refs),
        in_specs=[WHOLE] * 5,
        out_specs=WHOLE,
        scratch_shapes=[pltpu.VMEM((s, 2, n, r), F32)],
        out_shape=pltpu.VMEM((2, n, r), dtype),
        name="level",
        compiler_params=PARAMS,
    )(*[near(x) for x in operands])


def turn_kernel(ph_ref, out_ref):
    step = 16

    def body(j, carry):
        at = pl.ds(pl.multiple_of(j * step, step), step)
        c, s = cos_sin(ph_ref[at, :].astype(F32))
        out_ref[0, at, :] = c
        out_ref[1, at, :] = s
        return carry

    lax.fori_loop(0, ph_ref.shape[0] // step, body, 0)


def turns(ph):
    return pl.pallas_call(
        turn_kernel,
        in_specs=[WHOLE],
        out_specs=WHOLE,
        out_shape=pltpu.VMEM((2,) + ph.shape, F32),
        name="turns",
        compiler_params=PARAMS,
    )(near(ph))


def mixed(us, vs, i):
    lhs = [x for u in us for x in ((u[0], -u[1]) if i == 0 else (u[1], u[0]))]
    rhs = [v[j] for v in vs for j in (0, 1)]
    return tdot(jnp.concatenate(lhs, axis=0), jnp.concatenate(rhs, axis=0))


def gather_kernel(*refs):
    half = len(refs) // 2
    for i in (0, 1):
        refs[-1][i] = mixed(refs[:half], refs[half:-1], i)


def gathered(us, vs):
    _, _, m = us[0].shape
    _, _, r = vs[0].shape
    return pl.pallas_call(
        gather_kernel,
        in_specs=[WHOLE] * (2 * len(us)),
        out_specs=WHOLE,
        out_shape=pltpu.VMEM((2, m, r), F32),
        name="gathered",
        compiler_params=PARAMS,
    )(*[near(x) for x in us], *[near(x) for x in vs])


def image_kernel(u_ref, v_ref, part_ref, turn_ref, keep_ref, send_ref, acc_ref):
    own = core() == 0
    for i in (0, 1):
        acc_ref[i] = part_ref[i] + mixed((u_ref,), (v_ref,), i)

    def body(c, carry):
        x = c & 3
        z = c >> 2
        halves = []
        for h in (0, 1):
            at = pl.ds(pl.multiple_of(c * 64 + h * 32, 32), 32)
            co = turn_ref[0, at, :]
            si = turn_ref[1, at, :]
            re = acc_ref[0, at, :]
            im = acc_ref[1, at, :]
            halves.append((co * re - si * im, si * re + co * im))
        for i in (0, 1):
            keep_ref[x, z, i] = jnp.where(own, halves[0][i], halves[1][i])
            send_ref[x, z, i] = jnp.where(own, halves[1][i], halves[0][i]).astype(BF16)
        return carry

    lax.fori_loop(0, 8, body, 0)


def image_parts(u, v, part, turn):
    _, m, r = turn.shape
    shape = (4, 2, 2, m // 16, r)
    return pl.pallas_call(
        image_kernel,
        in_specs=[WHOLE] * 4,
        out_specs=[WHOLE, WHOLE],
        scratch_shapes=[pltpu.VMEM((2, m, r), F32)],
        out_shape=[pltpu.VMEM(shape, F32), pltpu.VMEM(shape, BF16)],
        name="image",
        compiler_params=PARAMS,
    )(near(u), near(v), near(part), near(turn))


def join_kernel(*refs):
    total = refs[0][...]
    for ref in refs[1:-1]:
        total += ref[...].astype(F32)
    refs[-1][...] = total.astype(BF16)


def join(first, *rest):
    return pl.pallas_call(
        join_kernel,
        in_specs=[WHOLE] * (1 + len(rest)),
        out_specs=WHOLE,
        out_shape=pltpu.VMEM(first.shape, BF16),
        name="join",
        compiler_params=PARAMS,
    )(*[near(x) for x in (first,) + rest])


def finish_kernel(*refs):
    for i in (0, 1):
        total = refs[0][i]
        for ref in refs[1:-1]:
            total += ref[i].astype(F32)
        refs[-1][:, i, :] = total


def finish(first, *rest):
    i, m, r = first.shape
    return pl.pallas_call(
        finish_kernel,
        in_specs=[WHOLE] * (1 + len(rest)),
        out_specs=WHOLE,
        out_shape=jax.ShapeDtypeStruct((m, i, r), F32),
        name="finish",
        compiler_params=PARAMS,
    )(*[near(x) for x in (first,) + rest])


def program(echoes, exponents, replica, interp0, upsample1, phase1, upsample2, phase2):
    fine = lax.axis_index("fine")
    coarse = lax.axis_index("coarse")
    y = fine // 2
    k = fine % 2
    cx = coarse % 4
    cz = coarse // 4
    range_bins = echoes.shape[3]

    expo = jnp.transpose(exponents, (0, 2, 1))
    u2_other = swap_cores(upsample2)
    u1_other = swap_cores(upsample1)
    even, odd = ends(echoes, expo)
    even = lax.ppermute(even, "swath", [(0, 1), (1, 0), (2, 3), (3, 2)])
    odd = lax.ppermute(odd, "swath", [(0, 0), (1, 2), (2, 1), (3, 3)])
    ph_own = jnp.transpose(phase1, (1, 0, 2))
    ph_other = swap_cores(ph_own)
    band = bands(replica)
    u2_parts = pack(upsample2, u2_other)
    samples = prep(echoes, expo)
    u2_parts = [u2_parts[0]] + [shift_chips(u2_parts[d], d) for d in (1, 2, 3)]

    b_own = beams_of(samples, even, odd, band, interp0)
    b_other = swap_cores(b_own)

    mix, ph_other = weights(upsample1, u1_other, ph_other)
    operands = (mix, ph_own, ph_other, b_own, b_other)
    received = [shift_chips(level_part(d, BF16, *operands), d) for d in (2, 1, 3)]
    total = level_part(0, F32, *operands)
    for part in received:
        total += part.astype(F32)
    level = total.astype(BF16)
    levels = [level] + [shift_chips(level, d) for d in (1, 2, 3)]

    ph2 = pick(pick(phase2.reshape(8, 4, 64, 2, range_bins), y, 1), k, 2).reshape(512, range_bins)
    turn = turns(ph2)

    keep, send = image_parts(u2_parts[3], levels[3], gathered(u2_parts[:3], levels[:3]), turn)
    other = swap_cores(send)
    narrow = (keep + other.astype(F32)).astype(BF16)

    def shares(z):
        first = pick(pick(keep, cx), z) + pick(pick(other, cx), z).astype(F32)
        return [first] + [shift_x(pick(pick(narrow, (cx + d) % 4), z), d) for d in (2, 1, 3)]

    far = swap_z(join(*shares(1 - cz)))
    return finish(*shares(cz), far)


def solution(mesh):
    in_specs = (
        P(("coarse", "fine"), None, None, "swath"),
        P(("coarse", "fine"), None, "swath"),
        P(),
        P(None, ("coarse", "fine"), None, None),
        P(None, ("coarse", "fine"), None, None),
        P(None, ("coarse", "fine"), "swath"),
        P("coarse", None, "fine", None),
        P(None, "coarse", "swath"),
    )
    out_specs = P(("coarse", "fine"), None, "swath")
    return jax.shard_map(program, mesh=mesh, in_specs=in_specs, out_specs=out_specs, check_vma=False)
```

profile of v0, /device:TPU:70, one launch (start us, length us, event | category | flops | bytes accessed | tf_op | source)
XLA Modules:
  0.0 77.9 jit_solution(10432646375350859585)
XLA Ops:
  0.0 2.1 %copy.13 = bf16[512,4,512]{2,0,1:T(8,128)(2,1)S(1)} copy(bf16[512,4,512]{2,1,0:T(4,128)(2,1)} %param.13) | data formatting | bytes 4194304 | tf_op args[5]
  4.0 1.9 %collective-permute-start.4 = (bf16[4,64,128]{2,1,0:T(8,128)(2,1)}, bf16[4,64,128]{2,1,0:T(8,128)(2,1)S(1)}, u32[]{:S(2)}, u32[]{:S(2)}) collective-permute-start(bf16[4,64,128]{2,1,0:T(8,128)(2,1)} %get-tuple-element.18), channel_id=1, source_target_pairs={{0,1},{1,0},{2,3},{3,2},{4,5},{5,4},{6,7},{7,6},{8,9},{9,8},{10,11... | collective-permute-start | bytes 196616 | tf_op jit(solution)/shard_map/ppermute | solution.py:448
  5.9 1.9 %collective-permute-start.5 = (bf16[4,64,128]{2,1,0:T(8,128)(2,1)S(1)}, bf16[4,64,128]{2,1,0:T(8,128)(2,1)S(1)}, u32[]{:S(2)}, u32[]{:S(2)}) collective-permute-start(bf16[4,64,128]{2,1,0:T(8,128)(2,1)S(1)} %get-tuple-element.19), channel_id=1, source_target_pairs={{0,0},{1,2},{2,1},{3,3},{4,4},{5,6},{6,5},{7,7},{8,8},{9,10},{10,9... | collective-permute-start | bytes 196616 | tf_op jit(solution)/shard_map/ppermute | solution.py:449
  8.9 3.1 %collective-permute-done.5.odd_ref = bf16[4,64,128]{2,1,0:T(8,128)(2,1)S(1)} collective-permute-done((bf16[4,64,128]{2,1,0:T(8,128)(2,1)S(1)}, bf16[4,64,128]{2,1,0:T(8,128)(2,1)S(1)}, u32[]{:S(2)}, u32[]{:S(2)}) %collective-permute-start.5) | collective-permute-done | bytes 65568 | tf_op jit(solution)/shard_map/ppermute | solution.py:449
  13.0 1.7 %weights.1 = (bf16[4,2,512,128]{3,2,1,0:T(8,128)(2,1)S(1)}, bf16[2,512,512]{2,1,0:T(8,128)(2,1)S(1)}) custom-call(bf16[2,4,64,512]{3,2,1,0:T(8,128)(2,1)} %u_own.1, bf16[2,4,64,512]{3,2,1,0:T(8,128)(2,1)} %collective-permute-done.2.u_other, bf16[4,512,512]{2,1,0:T(8,128)(2,1)} %collective-permute-done.3.ph_other), custom_call_target="tpu_custom_call" | custom-call | tf_op jit(solution)/shard_map/weights/pallas_call | solution.py:183
  14.8 1.5 %level.5 = bf16[2,128,512]{2,1,0:T(8,128)(2,1)S(1)} custom-call(bf16[4,2,512,128]{3,2,1,0:T(8,128)(2,1)S(1)} %get-tuple-element.16.refs_0_, bf16[4,512,512]{2,1,0:T(8,128)(2,1)S(1)} %bitcast.23, bf16[2,512,512]{2,1,0:T(8,128)(2,1)S(1)} %get-tuple-element.17.refs_2_, bf16[4,2,64,512]{3,2,1,0:T(8,128)(2,1)S(1)} %beams.1.refs_3_, ...), custom_call_target="tpu_custom_call" | custom-call | tf_op jit(solution)/shard_map/level/pallas_call | solution.py:299
  16.4 3.3 %collective-permute-start.7 = (bf16[2,128,512]{2,1,0:T(8,128)(2,1)S(1)}, bf16[2,128,512]{2,1,0:T(8,128)(2,1)S(1)}, u32[]{:S(2)}, u32[]{:S(2)}) collective-permute-start(bf16[2,128,512]{2,1,0:T(8,128)(2,1)S(1)} %level.5), channel_id=1, source_target_pairs={{0,16},{4,20},{8,24},{12,28},{16,0},{20,4},{24,8},{28,12},{1,17},{... | collective-permute-start | bytes 786440 | tf_op jit(solution)/shard_map/ppermute | solution.py:41
  19.7 1.5 %level.6 = bf16[2,128,512]{2,1,0:T(8,128)(2,1)S(1)} custom-call(bf16[4,2,512,128]{3,2,1,0:T(8,128)(2,1)S(1)} %get-tuple-element.16.refs_0_, bf16[4,512,512]{2,1,0:T(8,128)(2,1)S(1)} %bitcast.24, bf16[2,512,512]{2,1,0:T(8,128)(2,1)S(1)} %get-tuple-element.17.refs_2_, bf16[4,2,64,512]{3,2,1,0:T(8,128)(2,1)S(1)} %beams.1.refs_3_, ...), custom_call_target="tpu_custom_call" | custom-call | tf_op jit(solution)/shard_map/level/pallas_call | solution.py:299
  21.9 1.5 %level.7 = bf16[2,128,512]{2,1,0:T(8,128)(2,1)S(1)} custom-call(bf16[4,2,512,128]{3,2,1,0:T(8,128)(2,1)S(1)} %get-tuple-element.16.refs_0_, bf16[4,512,512]{2,1,0:T(8,128)(2,1)S(1)} %bitcast.25, bf16[2,512,512]{2,1,0:T(8,128)(2,1)S(1)} %get-tuple-element.17.refs_2_, bf16[4,2,64,512]{3,2,1,0:T(8,128)(2,1)S(1)} %beams.1.refs_3_, ...), custom_call_target="tpu_custom_call" | custom-call | tf_op jit(solution)/shard_map/level/pallas_call | solution.py:299
  23.5 2.6 %collective-permute-start.9 = (bf16[2,128,512]{2,1,0:T(8,128)(2,1)S(1)}, bf16[2,128,512]{2,1,0:T(8,128)(2,1)S(1)}, u32[]{:S(2)}, u32[]{:S(2)}) collective-permute-start(bf16[2,128,512]{2,1,0:T(8,128)(2,1)S(1)} %level.7), channel_id=1, source_target_pairs={{0,24},{4,28},{8,0},{12,4},{16,8},{20,12},{24,16},{28,20},{1,25},{... | collective-permute-start | bytes 786440 | tf_op jit(solution)/shard_map/ppermute | solution.py:41
  26.1 2.1 %pack.1 = (bf16[2,128,512]{2,1,0:T(8,128)(2,1)S(1)}, bf16[2,128,512]{2,1,0:T(8,128)(2,1)S(1)}, bf16[2,128,512]{2,1,0:T(8,128)(2,1)S(1)}, bf16[2,128,512]{2,1,0:T(8,128)(2,1)S(1)}) custom-call(bf16[2,2,64,2048]{3,2,1,0:T(8,128)(2,1)} %own_ref.1, bf16[2,2,64,2048]{3,2,1,0:T(8,128)(2,1)} %collective-permute-done.other_ref), custom_call_target="tpu_custom_call" | custom-call | tf_op jit(solution)/shard_map/pack/pallas_call | solution.py:156
  28.3 1.5 %collective-permute-start.12 = (bf16[2,128,512]{2,1,0:T(8,128)(2,1)S(1)}, bf16[2,128,512]{2,1,0:T(8,128)(2,1)S(1)}, u32[]{:S(2)}, u32[]{:S(2)}) collective-permute-start(bf16[2,128,512]{2,1,0:T(8,128)(2,1)S(1)} %get-tuple-element.22), channel_id=1, source_target_pairs={{0,16},{4,20},{8,24},{12,28},{16,0},{20,4},{24,8},{28,12},{1,17},{... | collective-permute-start | bytes 786440 | tf_op jit(solution)/shard_map/ppermute | solution.py:41
  29.8 1.5 %level.4 = f32[2,128,512]{2,1,0:T(8,128)S(1)} custom-call(bf16[4,2,512,128]{3,2,1,0:T(8,128)(2,1)S(1)} %get-tuple-element.16.refs_0_, bf16[4,512,512]{2,1,0:T(8,128)(2,1)S(1)} %bitcast.26, bf16[2,512,512]{2,1,0:T(8,128)(2,1)S(1)} %get-tuple-element.17.refs_2_, bf16[4,2,64,512]{3,2,1,0:T(8,128)(2,1)S(1)} %beams.1.refs_3_, ...), custom_call_target="tpu_custom_call" | custom-call | tf_op jit(solution)/shard_map/level/pallas_call | solution.py:299
  32.2 8.2 %collective-permute-done.9 = bf16[2,128,512]{2,1,0:T(8,128)(2,1)S(1)} collective-permute-done((bf16[2,128,512]{2,1,0:T(8,128)(2,1)S(1)}, bf16[2,128,512]{2,1,0:T(8,128)(2,1)S(1)}, u32[]{:S(2)}, u32[]{:S(2)}) %collective-permute-start.9) | collective-permute-done | bytes 262176 | tf_op jit(solution)/shard_map/ppermute | solution.py:41
  40.7 5.3 %collective-permute-start.14 = (bf16[2,128,512]{2,1,0:T(8,128)(2,1)S(1)}, bf16[2,128,512]{2,1,0:T(8,128)(2,1)S(1)}, u32[]{:S(2)}, u32[]{:S(2)}) collective-permute-start(bf16[2,128,512]{2,1,0:T(8,128)(2,1)S(1)} %add_convert_fusion.1.refs_3_), channel_id=1, source_target_pairs={{0,16},{4,20},{8,24},{12,28},{16,0},{20,4},{24,8},{28,12},{1,17},{... | collective-permute-start | bytes 786440 | tf_op jit(solution)/shard_map/ppermute | solution.py:41
  46.5 2.4 %constant_dynamic-slice_fusion = bf16[8,1,64,1,512]{4,3,2,1,0:T(2,128)(2,1)S(1)} fusion(bf16[8,4,64,2,512]{4,3,2,1,0:T(2,128)(2,1)} %bitcast.30, s32[]{:T(128)S(6)} %select_n.99, s32[]{:T(128)S(6)} %select_n.102), kind=kLoop, calls=%fused_computation.12 | loop fusion | bytes 1048584 | tf_op jit(solution)/shard_map/jit(dynamic_index_in_dim)/dynamic_slice | solution.py:53
  50.1 1.7 %collective-permute-done.13.refs_4_ = bf16[2,128,512]{2,1,0:T(8,128)(2,1)S(1)} collective-permute-done((bf16[2,128,512]{2,1,0:T(8,128)(2,1)S(1)}, bf16[2,128,512]{2,1,0:T(8,128)(2,1)S(1)}, u32[]{:S(2)}, u32[]{:S(2)}) %collective-permute-start.13) | collective-permute-done | bytes 262176 | tf_op jit(solution)/shard_map/ppermute | solution.py:41
  51.8 2.9 %collective-permute-done.14.refs_5_ = bf16[2,128,512]{2,1,0:T(8,128)(2,1)S(1)} collective-permute-done((bf16[2,128,512]{2,1,0:T(8,128)(2,1)S(1)}, bf16[2,128,512]{2,1,0:T(8,128)(2,1)S(1)}, u32[]{:S(2)}, u32[]{:S(2)}) %collective-permute-start.14) | collective-permute-done | bytes 262176 | tf_op jit(solution)/shard_map/ppermute | solution.py:41
  56.8 1.8 %collective-permute-done.15 = bf16[4,2,2,32,512]{4,3,2,1,0:T(8,128)(2,1)S(1)} collective-permute-done((bf16[4,2,2,32,512]{4,3,2,1,0:T(8,128)(2,1)S(1)}, bf16[4,2,2,32,512]{4,3,2,1,0:T(8,128)(2,1)S(1)}, u32[]{:S(2)}, u32[]{:S(2)}) %collective-permute-start.15) | collective-permute-done | bytes 524320 | tf_op jit(solution)/shard_map/ppermute | solution.py:37
  60.3 2.1 %collective-permute-start.20 = (bf16[2,32,512]{2,1,0:T(8,128)(2,1)S(1)}, bf16[2,32,512]{2,1,0:T(8,128)(2,1)S(1)}, u32[]{:S(2)}, u32[]{:S(2)}) collective-permute-start(bf16[2,32,512]{2,1,0:T(8,128)(2,1)S(1)} %get-tuple-element.28), channel_id=1, source_target_pairs={{0,32},{32,64},{64,96},{96,0},{128,160},{160,192},{192,224},{224,1... | collective-permute-start | bytes 196616 | tf_op jit(solution)/shard_map/ppermute | solution.py:45
  62.4 2.1 %collective-permute-start.16 = (bf16[2,32,512]{2,1,0:T(8,128)(2,1)S(1)}, bf16[2,32,512]{2,1,0:T(8,128)(2,1)S(1)}, u32[]{:S(2)}, u32[]{:S(2)}) collective-permute-start(bf16[2,32,512]{2,1,0:T(8,128)(2,1)S(1)} %get-tuple-element.32), channel_id=1, source_target_pairs={{0,64},{32,96},{64,0},{96,32},{128,192},{160,224},{192,128},{224,1... | collective-permute-start | bytes 196616 | tf_op jit(solution)/shard_map/ppermute | solution.py:45
  66.6 2.3 %collective-permute-done.21.refs_3_ = bf16[2,32,512]{2,1,0:T(8,128)(2,1)S(1)} collective-permute-done((bf16[2,32,512]{2,1,0:T(8,128)(2,1)S(1)}, bf16[2,32,512]{2,1,0:T(8,128)(2,1)S(1)}, u32[]{:S(2)}, u32[]{:S(2)}) %collective-permute-start.21) | collective-permute-done | bytes 65568 | tf_op jit(solution)/shard_map/ppermute | solution.py:45
  68.9 4.6 %collective-permute-start.22 = (bf16[2,32,512]{2,1,0:T(8,128)(2,1)S(1)}, bf16[2,32,512]{2,1,0:T(8,128)(2,1)S(1)}, u32[]{:S(2)}, u32[]{:S(2)}) collective-permute-start(bf16[2,32,512]{2,1,0:T(8,128)(2,1)S(1)} %join.1), channel_id=1, source_target_pairs={{0,128},{32,160},{64,192},{96,224},{128,0},{160,32},{192,64},{224,... | collective-permute-start | bytes 196616 | tf_op jit(solution)/shard_map/ppermute | solution.py:49
  73.5 3.7 %collective-permute-done.22.refs_4_ = bf16[2,32,512]{2,1,0:T(8,128)(2,1)S(1)} collective-permute-done((bf16[2,32,512]{2,1,0:T(8,128)(2,1)S(1)}, bf16[2,32,512]{2,1,0:T(8,128)(2,1)S(1)}, u32[]{:S(2)}, u32[]{:S(2)}) %collective-permute-start.22) | collective-permute-done | bytes 65568 | tf_op jit(solution)/shard_map/ppermute | solution.py:49
  (58 shorter events, 14.2 us)
Async XLA Ops:
  2.1 10.0 %copy-start.2 = (bf16[2,4,64,64]{3,2,1,0:T(8,128)(2,1)S(1)}, bf16[2,4,64,64]{3,2,1,0:T(8,128)(2,1)}, u32[]{:S(2)}) copy-start(bf16[2,4,64,64]{3,2,1,0:T(8,128)(2,1)} %w_ref.1) | copy-start | bytes 196612
  2.1 10.8 %collective-permute-start.3 = (bf16[4,512,512]{2,1,0:T(8,128)(2,1)S(1)}, bf16[4,512,512]{2,1,0:T(8,128)(2,1)}, u32[]{:S(2)}, u32[]{:S(2)}) collective-permute-start(bf16[4,512,512]{2,1,0:T(8,128)(2,1)S(1)} %bitcast.22), channel_id=1, source_target_pairs={{0,4},{4,0},{8,12},{12,8},{16,20},{20,16},{24,28},{28,24},{1,5},{5... | collective-permute-start | bytes 6291464 | tf_op jit(solution)/shard_map/ppermute | solution.py:37
  2.2 23.9 %collective-permute-start = (bf16[2,2,64,2048]{3,2,1,0:T(8,128)(2,1)}, bf16[2,2,64,2048]{3,2,1,0:T(8,128)(2,1)}, u32[]{:S(2)}, u32[]{:S(2)}) collective-permute-start(bf16[2,2,64,2048]{3,2,1,0:T(8,128)(2,1)} %own_ref.1), channel_id=1, source_target_pairs={{0,4},{4,0},{8,12},{12,8},{16,20},{20,16},{24,28},{28,24},{1,5},{5... | collective-permute-start | bytes 3145736 | tf_op jit(solution)/shard_map/ppermute | solution.py:37
  4.0 4.9 %collective-permute-start.4 = (bf16[4,64,128]{2,1,0:T(8,128)(2,1)}, bf16[4,64,128]{2,1,0:T(8,128)(2,1)S(1)}, u32[]{:S(2)}, u32[]{:S(2)}) collective-permute-start(bf16[4,64,128]{2,1,0:T(8,128)(2,1)} %get-tuple-element.18), channel_id=1, source_target_pairs={{0,1},{1,0},{2,3},{3,2},{4,5},{5,4},{6,7},{7,6},{8,9},{9,8},{10,11... | collective-permute-start | bytes 196616 | tf_op jit(solution)/shard_map/ppermute | solution.py:448
  5.9 6.1 %collective-permute-start.5 = (bf16[4,64,128]{2,1,0:T(8,128)(2,1)S(1)}, bf16[4,64,128]{2,1,0:T(8,128)(2,1)S(1)}, u32[]{:S(2)}, u32[]{:S(2)}) collective-permute-start(bf16[4,64,128]{2,1,0:T(8,128)(2,1)S(1)} %get-tuple-element.19), channel_id=1, source_target_pairs={{0,0},{1,2},{2,1},{3,3},{4,4},{5,6},{6,5},{7,7},{8,8},{9,10},{10,9... | collective-permute-start | bytes 196616 | tf_op jit(solution)/shard_map/ppermute | solution.py:449
  7.8 5.1 %collective-permute-start.2 = (bf16[2,4,64,512]{3,2,1,0:T(8,128)(2,1)}, bf16[2,4,64,512]{3,2,1,0:T(8,128)(2,1)}, u32[]{:S(2)}, u32[]{:S(2)}) collective-permute-start(bf16[2,4,64,512]{3,2,1,0:T(8,128)(2,1)} %u_own.1), channel_id=1, source_target_pairs={{0,4},{4,0},{8,12},{12,8},{16,20},{20,16},{24,28},{28,24},{1,5},{5... | collective-permute-start | bytes 1572872 | tf_op jit(solution)/shard_map/ppermute | solution.py:37
  12.8 2.0 %collective-permute-start.6 = (bf16[4,2,64,512]{3,2,1,0:T(8,128)(2,1)S(1)}, bf16[4,2,64,512]{3,2,1,0:T(8,128)(2,1)S(1)}, u32[]{:S(2)}, u32[]{:S(2)}) collective-permute-start(bf16[4,2,64,512]{3,2,1,0:T(8,128)(2,1)S(1)} %beams.1.refs_3_), channel_id=1, source_target_pairs={{0,4},{4,0},{8,12},{12,8},{16,20},{20,16},{24,28},{28,24},{1,5},{5... | collective-permute-start | bytes 1572872 | tf_op jit(solution)/shard_map/ppermute | solution.py:37
  16.4 15.0 %collective-permute-start.7 = (bf16[2,128,512]{2,1,0:T(8,128)(2,1)S(1)}, bf16[2,128,512]{2,1,0:T(8,128)(2,1)S(1)}, u32[]{:S(2)}, u32[]{:S(2)}) collective-permute-start(bf16[2,128,512]{2,1,0:T(8,128)(2,1)S(1)} %level.5), channel_id=1, source_target_pairs={{0,16},{4,20},{8,24},{12,28},{16,0},{20,4},{24,8},{28,12},{1,17},{... | collective-permute-start | bytes 786440 | tf_op jit(solution)/shard_map/ppermute | solution.py:41
  21.2 11.1 %collective-permute-start.8 = (bf16[2,128,512]{2,1,0:T(8,128)(2,1)S(1)}, bf16[2,128,512]{2,1,0:T(8,128)(2,1)S(1)}, u32[]{:S(2)}, u32[]{:S(2)}) collective-permute-start(bf16[2,128,512]{2,1,0:T(8,128)(2,1)S(1)} %level.6), channel_id=1, source_target_pairs={{0,8},{4,12},{8,16},{12,20},{16,24},{20,28},{24,0},{28,4},{1,9},{5... | collective-permute-start | bytes 786440 | tf_op jit(solution)/shard_map/ppermute | solution.py:41
  23.5 17.0 %collective-permute-start.9 = (bf16[2,128,512]{2,1,0:T(8,128)(2,1)S(1)}, bf16[2,128,512]{2,1,0:T(8,128)(2,1)S(1)}, u32[]{:S(2)}, u32[]{:S(2)}) collective-permute-start(bf16[2,128,512]{2,1,0:T(8,128)(2,1)S(1)} %level.7), channel_id=1, source_target_pairs={{0,24},{4,28},{8,0},{12,4},{16,8},{20,12},{24,16},{28,20},{1,25},{... | collective-permute-start | bytes 786440 | tf_op jit(solution)/shard_map/ppermute | solution.py:41
  28.2 17.7 %collective-permute-start.11 = (bf16[2,128,512]{2,1,0:T(8,128)(2,1)S(1)}, bf16[2,128,512]{2,1,0:T(8,128)(2,1)S(1)}, u32[]{:S(2)}, u32[]{:S(2)}) collective-permute-start(bf16[2,128,512]{2,1,0:T(8,128)(2,1)S(1)} %get-tuple-element.21), channel_id=1, source_target_pairs={{0,8},{4,12},{8,16},{12,20},{16,24},{20,28},{24,0},{28,4},{1,9},{5... | collective-permute-start | bytes 786440 | tf_op jit(solution)/shard_map/ppermute | solution.py:41
  28.3 21.8 %collective-permute-start.12 = (bf16[2,128,512]{2,1,0:T(8,128)(2,1)S(1)}, bf16[2,128,512]{2,1,0:T(8,128)(2,1)S(1)}, u32[]{:S(2)}, u32[]{:S(2)}) collective-permute-start(bf16[2,128,512]{2,1,0:T(8,128)(2,1)S(1)} %get-tuple-element.22), channel_id=1, source_target_pairs={{0,16},{4,20},{8,24},{12,28},{16,0},{20,4},{24,8},{28,12},{1,17},{... | collective-permute-start | bytes 786440 | tf_op jit(solution)/shard_map/ppermute | solution.py:41
  40.6 11.3 %collective-permute-start.13 = (bf16[2,128,512]{2,1,0:T(8,128)(2,1)S(1)}, bf16[2,128,512]{2,1,0:T(8,128)(2,1)S(1)}, u32[]{:S(2)}, u32[]{:S(2)}) collective-permute-start(bf16[2,128,512]{2,1,0:T(8,128)(2,1)S(1)} %add_convert_fusion.1.refs_3_), channel_id=1, source_target_pairs={{0,8},{4,12},{8,16},{12,20},{16,24},{20,28},{24,0},{28,4},{1,9},{5... | collective-permute-start | bytes 786440 | tf_op jit(solution)/shard_map/ppermute | solution.py:41
  40.7 14.1 %collective-permute-start.14 = (bf16[2,128,512]{2,1,0:T(8,128)(2,1)S(1)}, bf16[2,128,512]{2,1,0:T(8,128)(2,1)S(1)}, u32[]{:S(2)}, u32[]{:S(2)}) collective-permute-start(bf16[2,128,512]{2,1,0:T(8,128)(2,1)S(1)} %add_convert_fusion.1.refs_3_), channel_id=1, source_target_pairs={{0,16},{4,20},{8,24},{12,28},{16,0},{20,4},{24,8},{28,12},{1,17},{... | collective-permute-start | bytes 786440 | tf_op jit(solution)/shard_map/ppermute | solution.py:41
  45.9 9.8 %collective-permute-start.1 = (bf16[2,128,512]{2,1,0:T(8,128)(2,1)S(1)}, bf16[2,128,512]{2,1,0:T(8,128)(2,1)S(1)}, u32[]{:S(2)}, u32[]{:S(2)}) collective-permute-start(bf16[2,128,512]{2,1,0:T(8,128)(2,1)S(1)} %get-tuple-element.15), channel_id=1, source_target_pairs={{0,24},{4,28},{8,0},{12,4},{16,8},{20,12},{24,16},{28,20},{1,25},{... | collective-permute-start | bytes 786440 | tf_op jit(solution)/shard_map/ppermute | solution.py:41
  46.0 9.8 %collective-permute-start.10 = (bf16[2,128,512]{2,1,0:T(8,128)(2,1)S(1)}, bf16[2,128,512]{2,1,0:T(8,128)(2,1)S(1)}, u32[]{:S(2)}, u32[]{:S(2)}) collective-permute-start(bf16[2,128,512]{2,1,0:T(8,128)(2,1)S(1)} %add_convert_fusion.1.refs_3_), channel_id=1, source_target_pairs={{0,24},{4,28},{8,0},{12,4},{16,8},{20,12},{24,16},{28,20},{1,25},{... | collective-permute-start | bytes 786440 | tf_op jit(solution)/shard_map/ppermute | solution.py:41
  56.6 2.0 %collective-permute-start.15 = (bf16[4,2,2,32,512]{4,3,2,1,0:T(8,128)(2,1)S(1)}, bf16[4,2,2,32,512]{4,3,2,1,0:T(8,128)(2,1)S(1)}, u32[]{:S(2)}, u32[]{:S(2)}) collective-permute-start(bf16[4,2,2,32,512]{4,3,2,1,0:T(8,128)(2,1)S(1)} %get-tuple-element.24), channel_id=1, source_target_pairs={{0,4},{4,0},{8,12},{12,8},{16,20},{20,16},{24,28},{28,24},{1,5},{5... | collective-permute-start | bytes 1572872 | tf_op jit(solution)/shard_map/ppermute | solution.py:37
  58.8 6.9 %collective-permute-start.19 = (bf16[2,32,512]{2,1,0:T(8,128)(2,1)S(1)}, bf16[2,32,512]{2,1,0:T(8,128)(2,1)S(1)}, u32[]{:S(2)}, u32[]{:S(2)}) collective-permute-start(bf16[2,32,512]{2,1,0:T(8,128)(2,1)S(1)} %get-tuple-element.29), channel_id=1, source_target_pairs={{0,64},{32,96},{64,0},{96,32},{128,192},{160,224},{192,128},{224,1... | collective-permute-start | bytes 196616 | tf_op jit(solution)/shard_map/ppermute | solution.py:45
  60.3 6.3 %collective-permute-start.20 = (bf16[2,32,512]{2,1,0:T(8,128)(2,1)S(1)}, bf16[2,32,512]{2,1,0:T(8,128)(2,1)S(1)}, u32[]{:S(2)}, u32[]{:S(2)}) collective-permute-start(bf16[2,32,512]{2,1,0:T(8,128)(2,1)S(1)} %get-tuple-element.28), channel_id=1, source_target_pairs={{0,32},{32,64},{64,96},{96,0},{128,160},{160,192},{192,224},{224,1... | collective-permute-start | bytes 196616 | tf_op jit(solution)/shard_map/ppermute | solution.py:45
  62.4 6.5 %collective-permute-start.21 = (bf16[2,32,512]{2,1,0:T(8,128)(2,1)S(1)}, bf16[2,32,512]{2,1,0:T(8,128)(2,1)S(1)}, u32[]{:S(2)}, u32[]{:S(2)}) collective-permute-start(bf16[2,32,512]{2,1,0:T(8,128)(2,1)S(1)} %get-tuple-element.27), channel_id=1, source_target_pairs={{0,96},{32,0},{64,32},{96,64},{128,224},{160,128},{192,160},{224,1... | collective-permute-start | bytes 196616 | tf_op jit(solution)/shard_map/ppermute | solution.py:45
  62.4 11.1 %collective-permute-start.16 = (bf16[2,32,512]{2,1,0:T(8,128)(2,1)S(1)}, bf16[2,32,512]{2,1,0:T(8,128)(2,1)S(1)}, u32[]{:S(2)}, u32[]{:S(2)}) collective-permute-start(bf16[2,32,512]{2,1,0:T(8,128)(2,1)S(1)} %get-tuple-element.32), channel_id=1, source_target_pairs={{0,64},{32,96},{64,0},{96,32},{128,192},{160,224},{192,128},{224,1... | collective-permute-start | bytes 196616 | tf_op jit(solution)/shard_map/ppermute | solution.py:45
  64.5 9.0 %collective-permute-start.17 = (bf16[2,32,512]{2,1,0:T(8,128)(2,1)S(1)}, bf16[2,32,512]{2,1,0:T(8,128)(2,1)S(1)}, u32[]{:S(2)}, u32[]{:S(2)}) collective-permute-start(bf16[2,32,512]{2,1,0:T(8,128)(2,1)S(1)} %get-tuple-element.31), channel_id=1, source_target_pairs={{0,32},{32,64},{64,96},{96,0},{128,160},{160,192},{192,224},{224,1... | collective-permute-start | bytes 196616 | tf_op jit(solution)/shard_map/ppermute | solution.py:45
  65.7 7.8 %collective-permute-start.18 = (bf16[2,32,512]{2,1,0:T(8,128)(2,1)S(1)}, bf16[2,32,512]{2,1,0:T(8,128)(2,1)S(1)}, u32[]{:S(2)}, u32[]{:S(2)}) collective-permute-start(bf16[2,32,512]{2,1,0:T(8,128)(2,1)S(1)} %get-tuple-element.30), channel_id=1, source_target_pairs={{0,96},{32,0},{64,32},{96,64},{128,224},{160,128},{192,160},{224,1... | collective-permute-start | bytes 196616 | tf_op jit(solution)/shard_map/ppermute | solution.py:45
  68.9 8.3 %collective-permute-start.22 = (bf16[2,32,512]{2,1,0:T(8,128)(2,1)S(1)}, bf16[2,32,512]{2,1,0:T(8,128)(2,1)S(1)}, u32[]{:S(2)}, u32[]{:S(2)}) collective-permute-start(bf16[2,32,512]{2,1,0:T(8,128)(2,1)S(1)} %join.1), channel_id=1, source_target_pairs={{0,128},{32,160},{64,192},{96,224},{128,0},{160,32},{192,64},{224,... | collective-permute-start | bytes 196616 | tf_op jit(solution)/shard_map/ppermute | solution.py:49
  (3 other events, 11.3 us)
where the time goes:
time: 78.1 us; the launch traced here: 77.9 us
  starting transfers between devices  31.2 us (40%)
  waiting for transfers between devices  24.7 us (32%)
  Pallas kernels  16.3 us (21%)
  local copies, waits for them, and re-layouts  4.91 us (6%)
    ppermute x9, starting transfers between devices, shift_chips(): lax.ppermute(x, 'fine', [(y * 2 + k, (y + d) % 4 * 2 + k) for y in range(...  14.2 us
    ppermute x9, waiting for transfers between devices, shift_chips(): lax.ppermute(x, 'fine', [(y * 2 + k, (y + d) % 4 * 2 + k) for y in range(...  13.7 us
    ppermute x6, starting transfers between devices, shift_x(): lax.ppermute(x, 'coarse', [(z * 4 + i, z * 4 + (i + d) % 4) for z in rang...  7.75 us
    pallas_call x4, Pallas kernels, level_part(): pl.pallas_call(lambda *refs: level_kernel(d, *refs), in_specs=[WHOLE] * 5...  6.07 us
    ppermute x1, starting transfers between devices, swap_z(): return lax.ppermute(x, 'coarse', [(i, i ^ 4) for i in range(8)])  4.58 us
    ppermute x1, waiting for transfers between devices, swap_z(): return lax.ppermute(x, 'coarse', [(i, i ^ 4) for i in range(8)])  3.67 us
    ppermute x1, waiting for transfers between devices, program(): odd = lax.ppermute(odd, 'swath', [(0, 0), (1, 2), (2, 1), (3, 3)])  3.12 us
    dynamic_slice x1, local copies, waits for them, and re-layouts, pick(): return lax.dynamic_index_in_dim(x, i, axis, keepdims=False)  2.39 us
  transfers between devices with their start and end apart: 23, of which 9 were waited for; matrix products, arithmetic and copies ran while one was open for 4% of the time, Pallas kernels for 19%

commit v1 on v0

--- a/solution.py
+++ b/solution.py
@@ -356,10 +356,11 @@
     )(*[near(x) for x in us], *[near(x) for x in vs])
 
 
-def image_kernel(u_ref, v_ref, part_ref, turn_ref, keep_ref, send_ref, acc_ref):
+def image_kernel(u_ref, low_ref, high_ref, part_ref, turn_ref, keep_ref, send_ref, acc_ref):
     own = core() == 0
+    v = [jnp.concatenate([low_ref[j], high_ref[j]], axis=0) for j in (0, 1)]
     for i in (0, 1):
-        acc_ref[i] = part_ref[i] + mixed((u_ref,), (v_ref,), i)
+        acc_ref[i] = part_ref[i] + mixed((u_ref,), (v,), i)
 
     def body(c, carry):
         x = c & 3
@@ -380,18 +381,18 @@
     lax.fori_loop(0, 8, body, 0)
 
 
-def image_parts(u, v, part, turn):
+def image_parts(u, low, high, part, turn):
     _, m, r = turn.shape
     shape = (4, 2, 2, m // 16, r)
     return pl.pallas_call(
         image_kernel,
-        in_specs=[WHOLE] * 4,
+        in_specs=[WHOLE] * 5,
         out_specs=[WHOLE, WHOLE],
         scratch_shapes=[pltpu.VMEM((2, m, r), F32)],
         out_shape=[pltpu.VMEM(shape, F32), pltpu.VMEM(shape, BF16)],
         name="image",
         compiler_params=PARAMS,
-    )(near(u), near(v), near(part), near(turn))
+    )(near(u), near(low), near(high), near(part), near(turn))
 
 
 def join_kernel(*refs):
@@ -464,12 +465,18 @@
     for part in received:
         total += part.astype(F32)
     level = total.astype(BF16)
-    levels = [level] + [shift_chips(level, d) for d in (1, 2, 3)]
+    before = shift_chips(level, 1)
+    after = shift_chips(level, 3)
+    half = level.shape[1] // 2
+    low = shift_chips(before[:, :half], 1)
+    high = shift_chips(after[:, half:], 3)
 
     ph2 = pick(pick(phase2.reshape(8, 4, 64, 2, range_bins), y, 1), k, 2).reshape(512, range_bins)
     turn = turns(ph2)
 
-    keep, send = image_parts(u2_parts[3], levels[3], gathered(u2_parts[:3], levels[:3]), turn)
+    keep, send = image_parts(
+        u2_parts[2], low, high, gathered([u2_parts[0], u2_parts[1], u2_parts[3]], [level, before, after]), turn
+    )
     other = swap_cores(send)
     narrow = (keep + other.astype(F32)).astype(BF16)
 

time: 78.1 us -> 78.1 us (level)
  the two profiles are of different devices: /device:TPU:70 before, /device:TPU:38 now
where the time goes in v1:
time: 78.1 us; the launch traced here: 77.9 us
  starting transfers between devices  37 us (47%)
  waiting for transfers between devices  20 us (26%)
  Pallas kernels  15.2 us (19%)
  local copies, waits for them, and re-layouts  4.93 us (6%)
    ppermute x10, starting transfers between devices, shift_chips(): lax.ppermute(x, 'fine', [(y * 2 + k, (y + d) % 4 * 2 + k) for y in range(...  17.3 us
    ppermute x10, waiting for transfers between devices, shift_chips(): lax.ppermute(x, 'fine', [(y * 2 + k, (y + d) % 4 * 2 + k) for y in range(...  11.7 us
    ppermute x6, starting transfers between devices, shift_x(): lax.ppermute(x, 'coarse', [(z * 4 + i, z * 4 + (i + d) % 4) for z in rang...  7.76 us
    pallas_call x4, Pallas kernels, level_part(): pl.pallas_call(lambda *refs: level_kernel(d, *refs), in_specs=[WHOLE] * 5...  6.07 us
    ppermute x1, starting transfers between devices, program(): odd = lax.ppermute(odd, 'swath', [(0, 0), (1, 2), (2, 1), (3, 3)])  5.62 us
    ppermute x1, starting transfers between devices, swap_z(): return lax.ppermute(x, 'coarse', [(i, i ^ 4) for i in range(8)])  5.35 us
    ppermute x1, waiting for transfers between devices, swap_z(): return lax.ppermute(x, 'coarse', [(i, i ^ 4) for i in range(8)])  2.89 us
    dynamic_slice x1, local copies, waits for them, and re-layouts, pick(): return lax.dynamic_index_in_dim(x, i, axis, keepdims=False)  2.39 us
  transfers between devices with their start and end apart: 24, of which 12 were waited for; matrix products, arithmetic and copies ran while one was open for 4% of the time, Pallas kernels for 18%

profile of v1, /device:TPU:38, one launch (start us, length us, event | category | flops | bytes accessed | tf_op | source)
XLA Modules:
  0.0 77.9 jit_solution(9562594198276857214)
XLA Ops:
  0.0 2.1 %copy.13 = bf16[512,4,512]{2,0,1:T(8,128)(2,1)S(1)} copy(bf16[512,4,512]{2,1,0:T(4,128)(2,1)} %param.13) | data formatting | bytes 4194304 | tf_op args[5]
  3.6 5.6 %collective-permute-start.5 = (bf16[4,64,128]{2,1,0:T(8,128)(2,1)S(1)}, bf16[4,64,128]{2,1,0:T(8,128)(2,1)S(1)}, u32[]{:S(2)}, u32[]{:S(2)}) collective-permute-start(bf16[4,64,128]{2,1,0:T(8,128)(2,1)S(1)} %get-tuple-element.19), channel_id=1, source_target_pairs={{0,0},{1,2},{2,1},{3,3},{4,4},{5,6},{6,5},{7,7},{8,8},{9,10},{10,9... | collective-permute-start | bytes 196616 | tf_op jit(solution)/shard_map/ppermute | solution.py:450
  13.1 1.7 %weights.1 = (bf16[4,2,512,128]{3,2,1,0:T(8,128)(2,1)S(1)}, bf16[2,512,512]{2,1,0:T(8,128)(2,1)S(1)}) custom-call(bf16[2,4,64,512]{3,2,1,0:T(8,128)(2,1)} %u_own.1, bf16[2,4,64,512]{3,2,1,0:T(8,128)(2,1)} %collective-permute-done.2.u_other, bf16[4,512,512]{2,1,0:T(8,128)(2,1)} %collective-permute-done.3.ph_other), custom_call_target="tpu_custom_call" | custom-call | tf_op jit(solution)/shard_map/weights/pallas_call | solution.py:183
  14.8 1.5 %level.5 = bf16[2,128,512]{2,1,0:T(8,128)(2,1)S(1)} custom-call(bf16[4,2,512,128]{3,2,1,0:T(8,128)(2,1)S(1)} %get-tuple-element.16.refs_0_, bf16[4,512,512]{2,1,0:T(8,128)(2,1)S(1)} %bitcast.23, bf16[2,512,512]{2,1,0:T(8,128)(2,1)S(1)} %get-tuple-element.17.refs_2_, bf16[4,2,64,512]{3,2,1,0:T(8,128)(2,1)S(1)} %beams.1.refs_3_, ...), custom_call_target="tpu_custom_call" | custom-call | tf_op jit(solution)/shard_map/level/pallas_call | solution.py:299
  16.4 3.3 %collective-permute-start.7 = (bf16[2,128,512]{2,1,0:T(8,128)(2,1)S(1)}, bf16[2,128,512]{2,1,0:T(8,128)(2,1)S(1)}, u32[]{:S(2)}, u32[]{:S(2)}) collective-permute-start(bf16[2,128,512]{2,1,0:T(8,128)(2,1)S(1)} %level.5), channel_id=1, source_target_pairs={{0,16},{4,20},{8,24},{12,28},{16,0},{20,4},{24,8},{28,12},{1,17},{... | collective-permute-start | bytes 786440 | tf_op jit(solution)/shard_map/ppermute | solution.py:41
  19.7 1.5 %level.6 = bf16[2,128,512]{2,1,0:T(8,128)(2,1)S(1)} custom-call(bf16[4,2,512,128]{3,2,1,0:T(8,128)(2,1)S(1)} %get-tuple-element.16.refs_0_, bf16[4,512,512]{2,1,0:T(8,128)(2,1)S(1)} %bitcast.24, bf16[2,512,512]{2,1,0:T(8,128)(2,1)S(1)} %get-tuple-element.17.refs_2_, bf16[4,2,64,512]{3,2,1,0:T(8,128)(2,1)S(1)} %beams.1.refs_3_, ...), custom_call_target="tpu_custom_call" | custom-call | tf_op jit(solution)/shard_map/level/pallas_call | solution.py:299
  21.9 1.5 %level.7 = bf16[2,128,512]{2,1,0:T(8,128)(2,1)S(1)} custom-call(bf16[4,2,512,128]{3,2,1,0:T(8,128)(2,1)S(1)} %get-tuple-element.16.refs_0_, bf16[4,512,512]{2,1,0:T(8,128)(2,1)S(1)} %bitcast.25, bf16[2,512,512]{2,1,0:T(8,128)(2,1)S(1)} %get-tuple-element.17.refs_2_, bf16[4,2,64,512]{3,2,1,0:T(8,128)(2,1)S(1)} %beams.1.refs_3_, ...), custom_call_target="tpu_custom_call" | custom-call | tf_op jit(solution)/shard_map/level/pallas_call | solution.py:299
  23.5 2.6 %collective-permute-start.9 = (bf16[2,128,512]{2,1,0:T(8,128)(2,1)S(1)}, bf16[2,128,512]{2,1,0:T(8,128)(2,1)S(1)}, u32[]{:S(2)}, u32[]{:S(2)}) collective-permute-start(bf16[2,128,512]{2,1,0:T(8,128)(2,1)S(1)} %level.7), channel_id=1, source_target_pairs={{0,24},{4,28},{8,0},{12,4},{16,8},{20,12},{24,16},{28,20},{1,25},{... | collective-permute-start | bytes 786440 | tf_op jit(solution)/shard_map/ppermute | solution.py:41
  26.1 1.5 %level.4 = f32[2,128,512]{2,1,0:T(8,128)S(1)} custom-call(bf16[4,2,512,128]{3,2,1,0:T(8,128)(2,1)S(1)} %get-tuple-element.16.refs_0_, bf16[4,512,512]{2,1,0:T(8,128)(2,1)S(1)} %bitcast.26, bf16[2,512,512]{2,1,0:T(8,128)(2,1)S(1)} %get-tuple-element.17.refs_2_, bf16[4,2,64,512]{3,2,1,0:T(8,128)(2,1)S(1)} %beams.1.refs_3_, ...), custom_call_target="tpu_custom_call" | custom-call | tf_op jit(solution)/shard_map/level/pallas_call | solution.py:299
  27.6 4.3 %collective-permute-done.8 = bf16[2,128,512]{2,1,0:T(8,128)(2,1)S(1)} collective-permute-done((bf16[2,128,512]{2,1,0:T(8,128)(2,1)S(1)}, bf16[2,128,512]{2,1,0:T(8,128)(2,1)S(1)}, u32[]{:S(2)}, u32[]{:S(2)}) %collective-permute-start.8) | collective-permute-done | bytes 262176 | tf_op jit(solution)/shard_map/ppermute | solution.py:41
  32.4 1.5 %collective-permute-start.10 = (bf16[2,128,512]{2,1,0:T(8,128)(2,1)S(1)}, bf16[2,128,512]{2,1,0:T(8,128)(2,1)S(1)}, u32[]{:S(2)}, u32[]{:S(2)}) collective-permute-start(bf16[2,128,512]{2,1,0:T(8,128)(2,1)S(1)} %add_convert_fusion.1.refs_3_), channel_id=1, source_target_pairs={{0,8},{4,12},{8,16},{12,20},{16,24},{20,28},{24,0},{28,4},{1,9},{5... | collective-permute-start | bytes 786440 | tf_op jit(solution)/shard_map/ppermute | solution.py:41
  33.9 1.9 %collective-permute-start.12 = (bf16[2,128,512]{2,1,0:T(8,128)(2,1)S(1)}, bf16[2,128,512]{2,1,0:T(8,128)(2,1)S(1)}, u32[]{:S(2)}, u32[]{:S(2)}) collective-permute-start(bf16[2,128,512]{2,1,0:T(8,128)(2,1)S(1)} %add_convert_fusion.1.refs_3_), channel_id=1, source_target_pairs={{0,24},{4,28},{8,0},{12,4},{16,8},{20,12},{24,16},{28,20},{1,25},{... | collective-permute-start | bytes 786440 | tf_op jit(solution)/shard_map/ppermute | solution.py:41
  37.2 3.1 %collective-permute-start.15 = (bf16[2,128,512]{2,1,0:T(8,128)(2,1)S(1)}, bf16[2,128,512]{2,1,0:T(8,128)(2,1)S(1)}, u32[]{:S(2)}, u32[]{:S(2)}) collective-permute-start(bf16[2,128,512]{2,1,0:T(8,128)(2,1)S(1)} %get-tuple-element.22), channel_id=1, source_target_pairs={{0,24},{4,28},{8,0},{12,4},{16,8},{20,12},{24,16},{28,20},{1,25},{... | collective-permute-start | bytes 786440 | tf_op jit(solution)/shard_map/ppermute | solution.py:41
  40.7 2.2 %collective-permute-done.10.refs_4_ = bf16[2,128,512]{2,1,0:T(8,128)(2,1)S(1)} collective-permute-done((bf16[2,128,512]{2,1,0:T(8,128)(2,1)S(1)}, bf16[2,128,512]{2,1,0:T(8,128)(2,1)S(1)}, u32[]{:S(2)}, u32[]{:S(2)}) %collective-permute-start.10) | collective-permute-done | bytes 262176 | tf_op jit(solution)/shard_map/ppermute | solution.py:41
  43.1 3.1 %collective-permute-start.13 = (bf16[2,64,512]{2,1,0:T(8,128)(2,1)S(1)}, bf16[2,64,512]{2,1,0:T(8,128)(2,1)S(1)}, u32[]{:S(2)}, u32[]{:S(2)}) collective-permute-start(bf16[2,64,512]{2,1,0:T(8,128)(2,1)S(1)} %slice.19), channel_id=1, source_target_pairs={{0,24},{4,28},{8,0},{12,4},{16,8},{20,12},{24,16},{28,20},{1,25},{... | collective-permute-start | bytes 393224 | tf_op jit(solution)/shard_map/ppermute | solution.py:41
  46.3 2.4 %constant_dynamic-slice_fusion = bf16[8,1,64,1,512]{4,3,2,1,0:T(2,128)(2,1)S(1)} fusion(bf16[8,4,64,2,512]{4,3,2,1,0:T(2,128)(2,1)} %bitcast.30, s32[]{:T(128)S(6)} %select_n.99, s32[]{:T(128)S(6)} %select_n.102), kind=kLoop, calls=%fused_computation.12 | loop fusion | bytes 1048584 | tf_op jit(solution)/shard_map/jit(dynamic_index_in_dim)/dynamic_slice | solution.py:53
  49.8 2.6 %collective-permute-done.14.refs_1_ = bf16[2,128,512]{2,1,0:T(8,128)(2,1)S(1)} collective-permute-done((bf16[2,128,512]{2,1,0:T(8,128)(2,1)S(1)}, bf16[2,128,512]{2,1,0:T(8,128)(2,1)S(1)}, u32[]{:S(2)}, u32[]{:S(2)}) %collective-permute-start.14) | collective-permute-done | bytes 262176 | tf_op jit(solution)/shard_map/ppermute | solution.py:41
  56.8 1.8 %collective-permute-done.16 = bf16[4,2,2,32,512]{4,3,2,1,0:T(8,128)(2,1)S(1)} collective-permute-done((bf16[4,2,2,32,512]{4,3,2,1,0:T(8,128)(2,1)S(1)}, bf16[4,2,2,32,512]{4,3,2,1,0:T(8,128)(2,1)S(1)}, u32[]{:S(2)}, u32[]{:S(2)}) %collective-permute-start.16) | collective-permute-done | bytes 524320 | tf_op jit(solution)/shard_map/ppermute | solution.py:37
  58.8 1.5 %collective-permute-start.20 = (bf16[2,32,512]{2,1,0:T(8,128)(2,1)S(1)}, bf16[2,32,512]{2,1,0:T(8,128)(2,1)S(1)}, u32[]{:S(2)}, u32[]{:S(2)}) collective-permute-start(bf16[2,32,512]{2,1,0:T(8,128)(2,1)S(1)} %get-tuple-element.29), channel_id=1, source_target_pairs={{0,64},{32,96},{64,0},{96,32},{128,192},{160,224},{192,128},{224,1... | collective-permute-start | bytes 196616 | tf_op jit(solution)/shard_map/ppermute | solution.py:45
  60.3 2.1 %collective-permute-start.21 = (bf16[2,32,512]{2,1,0:T(8,128)(2,1)S(1)}, bf16[2,32,512]{2,1,0:T(8,128)(2,1)S(1)}, u32[]{:S(2)}, u32[]{:S(2)}) collective-permute-start(bf16[2,32,512]{2,1,0:T(8,128)(2,1)S(1)} %get-tuple-element.28), channel_id=1, source_target_pairs={{0,32},{32,64},{64,96},{96,0},{128,160},{160,192},{192,224},{224,1... | collective-permute-start | bytes 196616 | tf_op jit(solution)/shard_map/ppermute | solution.py:45
  62.4 2.1 %collective-permute-start.17 = (bf16[2,32,512]{2,1,0:T(8,128)(2,1)S(1)}, bf16[2,32,512]{2,1,0:T(8,128)(2,1)S(1)}, u32[]{:S(2)}, u32[]{:S(2)}) collective-permute-start(bf16[2,32,512]{2,1,0:T(8,128)(2,1)S(1)} %get-tuple-element.32), channel_id=1, source_target_pairs={{0,64},{32,96},{64,0},{96,32},{128,192},{160,224},{192,128},{224,1... | collective-permute-start | bytes 196616 | tf_op jit(solution)/shard_map/ppermute | solution.py:45
  66.6 2.3 %collective-permute-done.22.refs_3_ = bf16[2,32,512]{2,1,0:T(8,128)(2,1)S(1)} collective-permute-done((bf16[2,32,512]{2,1,0:T(8,128)(2,1)S(1)}, bf16[2,32,512]{2,1,0:T(8,128)(2,1)S(1)}, u32[]{:S(2)}, u32[]{:S(2)}) %collective-permute-start.22) | collective-permute-done | bytes 65568 | tf_op jit(solution)/shard_map/ppermute | solution.py:45
  68.9 5.4 %collective-permute-start.23 = (bf16[2,32,512]{2,1,0:T(8,128)(2,1)S(1)}, bf16[2,32,512]{2,1,0:T(8,128)(2,1)S(1)}, u32[]{:S(2)}, u32[]{:S(2)}) collective-permute-start(bf16[2,32,512]{2,1,0:T(8,128)(2,1)S(1)} %join.1), channel_id=1, source_target_pairs={{0,128},{32,160},{64,192},{96,224},{128,0},{160,32},{192,64},{224,... | collective-permute-start | bytes 196616 | tf_op jit(solution)/shard_map/ppermute | solution.py:49
  74.3 2.9 %collective-permute-done.23.refs_4_ = bf16[2,32,512]{2,1,0:T(8,128)(2,1)S(1)} collective-permute-done((bf16[2,32,512]{2,1,0:T(8,128)(2,1)S(1)}, bf16[2,32,512]{2,1,0:T(8,128)(2,1)S(1)}, u32[]{:S(2)}, u32[]{:S(2)}) %collective-permute-start.23) | collective-permute-done | bytes 65568 | tf_op jit(solution)/shard_map/ppermute | solution.py:49
  (64 shorter events, 17.1 us)
Async XLA Ops:
  2.1 11.0 %collective-permute-start.3 = (bf16[4,512,512]{2,1,0:T(8,128)(2,1)S(1)}, bf16[4,512,512]{2,1,0:T(8,128)(2,1)}, u32[]{:S(2)}, u32[]{:S(2)}) collective-permute-start(bf16[4,512,512]{2,1,0:T(8,128)(2,1)S(1)} %bitcast.22), channel_id=1, source_target_pairs={{0,4},{4,0},{8,12},{12,8},{16,20},{20,16},{24,28},{28,24},{1,5},{5... | collective-permute-start | bytes 6291464 | tf_op jit(solution)/shard_map/ppermute | solution.py:37
  3.5 6.8 %collective-permute-start.4 = (bf16[4,64,128]{2,1,0:T(8,128)(2,1)}, bf16[4,64,128]{2,1,0:T(8,128)(2,1)S(1)}, u32[]{:S(2)}, u32[]{:S(2)}) collective-permute-start(bf16[4,64,128]{2,1,0:T(8,128)(2,1)} %get-tuple-element.18), channel_id=1, source_target_pairs={{0,1},{1,0},{2,3},{3,2},{4,5},{5,4},{6,7},{7,6},{8,9},{9,8},{10,11... | collective-permute-start | bytes 196616 | tf_op jit(solution)/shard_map/ppermute | solution.py:449
  3.6 8.1 %collective-permute-start.5 = (bf16[4,64,128]{2,1,0:T(8,128)(2,1)S(1)}, bf16[4,64,128]{2,1,0:T(8,128)(2,1)S(1)}, u32[]{:S(2)}, u32[]{:S(2)}) collective-permute-start(bf16[4,64,128]{2,1,0:T(8,128)(2,1)S(1)} %get-tuple-element.19), channel_id=1, source_target_pairs={{0,0},{1,2},{2,1},{3,3},{4,4},{5,6},{6,5},{7,7},{8,8},{9,10},{10,9... | collective-permute-start | bytes 196616 | tf_op jit(solution)/shard_map/ppermute | solution.py:450
  9.3 3.8 %collective-permute-start.2 = (bf16[2,4,64,512]{3,2,1,0:T(8,128)(2,1)}, bf16[2,4,64,512]{3,2,1,0:T(8,128)(2,1)}, u32[]{:S(2)}, u32[]{:S(2)}) collective-permute-start(bf16[2,4,64,512]{3,2,1,0:T(8,128)(2,1)} %u_own.1), channel_id=1, source_target_pairs={{0,4},{4,0},{8,12},{12,8},{16,20},{20,16},{24,28},{28,24},{1,5},{5... | collective-permute-start | bytes 1572872 | tf_op jit(solution)/shard_map/ppermute | solution.py:37
  12.5 2.3 %collective-permute-start.6 = (bf16[4,2,64,512]{3,2,1,0:T(8,128)(2,1)S(1)}, bf16[4,2,64,512]{3,2,1,0:T(8,128)(2,1)S(1)}, u32[]{:S(2)}, u32[]{:S(2)}) collective-permute-start(bf16[4,2,64,512]{3,2,1,0:T(8,128)(2,1)S(1)} %beams.1.refs_3_), channel_id=1, source_target_pairs={{0,4},{4,0},{8,12},{12,8},{16,20},{20,16},{24,28},{28,24},{1,5},{5... | collective-permute-start | bytes 1572872 | tf_op jit(solution)/shard_map/ppermute | solution.py:37
  12.6 23.1 %collective-permute-start = (bf16[2,2,64,2048]{3,2,1,0:T(8,128)(2,1)S(1)}, bf16[2,2,64,2048]{3,2,1,0:T(8,128)(2,1)S(1)}, u32[]{:S(2)}, u32[]{:S(2)}) collective-permute-start(bf16[2,2,64,2048]{3,2,1,0:T(8,128)(2,1)S(1)} %copy-done.1), channel_id=1, source_target_pairs={{0,4},{4,0},{8,12},{12,8},{16,20},{20,16},{24,28},{28,24},{1,5},{5... | collective-permute-start | bytes 3145736 | tf_op jit(solution)/shard_map/ppermute | solution.py:37
  16.4 11.3 %collective-permute-start.7 = (bf16[2,128,512]{2,1,0:T(8,128)(2,1)S(1)}, bf16[2,128,512]{2,1,0:T(8,128)(2,1)S(1)}, u32[]{:S(2)}, u32[]{:S(2)}) collective-permute-start(bf16[2,128,512]{2,1,0:T(8,128)(2,1)S(1)} %level.5), channel_id=1, source_target_pairs={{0,16},{4,20},{8,24},{12,28},{16,0},{20,4},{24,8},{28,12},{1,17},{... | collective-permute-start | bytes 786440 | tf_op jit(solution)/shard_map/ppermute | solution.py:41
  21.2 10.7 %collective-permute-start.8 = (bf16[2,128,512]{2,1,0:T(8,128)(2,1)S(1)}, bf16[2,128,512]{2,1,0:T(8,128)(2,1)S(1)}, u32[]{:S(2)}, u32[]{:S(2)}) collective-permute-start(bf16[2,128,512]{2,1,0:T(8,128)(2,1)S(1)} %level.6), channel_id=1, source_target_pairs={{0,8},{4,12},{8,16},{12,20},{16,24},{20,28},{24,0},{28,4},{1,9},{5... | collective-permute-start | bytes 786440 | tf_op jit(solution)/shard_map/ppermute | solution.py:41
  23.5 8.8 %collective-permute-start.9 = (bf16[2,128,512]{2,1,0:T(8,128)(2,1)S(1)}, bf16[2,128,512]{2,1,0:T(8,128)(2,1)S(1)}, u32[]{:S(2)}, u32[]{:S(2)}) collective-permute-start(bf16[2,128,512]{2,1,0:T(8,128)(2,1)S(1)} %level.7), channel_id=1, source_target_pairs={{0,24},{4,28},{8,0},{12,4},{16,8},{20,12},{24,16},{28,20},{1,25},{... | collective-permute-start | bytes 786440 | tf_op jit(solution)/shard_map/ppermute | solution.py:41
  32.4 10.5 %collective-permute-start.10 = (bf16[2,128,512]{2,1,0:T(8,128)(2,1)S(1)}, bf16[2,128,512]{2,1,0:T(8,128)(2,1)S(1)}, u32[]{:S(2)}, u32[]{:S(2)}) collective-permute-start(bf16[2,128,512]{2,1,0:T(8,128)(2,1)S(1)} %add_convert_fusion.1.refs_3_), channel_id=1, source_target_pairs={{0,8},{4,12},{8,16},{12,20},{16,24},{20,28},{24,0},{28,4},{1,9},{5... | collective-permute-start | bytes 786440 | tf_op jit(solution)/shard_map/ppermute | solution.py:41
  33.9 9.3 %collective-permute-start.12 = (bf16[2,128,512]{2,1,0:T(8,128)(2,1)S(1)}, bf16[2,128,512]{2,1,0:T(8,128)(2,1)S(1)}, u32[]{:S(2)}, u32[]{:S(2)}) collective-permute-start(bf16[2,128,512]{2,1,0:T(8,128)(2,1)S(1)} %add_convert_fusion.1.refs_3_), channel_id=1, source_target_pairs={{0,24},{4,28},{8,0},{12,4},{16,8},{20,12},{24,16},{28,20},{1,25},{... | collective-permute-start | bytes 786440 | tf_op jit(solution)/shard_map/ppermute | solution.py:41
  36.8 15.7 %collective-permute-start.14 = (bf16[2,128,512]{2,1,0:T(8,128)(2,1)S(1)}, bf16[2,128,512]{2,1,0:T(8,128)(2,1)S(1)}, u32[]{:S(2)}, u32[]{:S(2)}) collective-permute-start(bf16[2,128,512]{2,1,0:T(8,128)(2,1)S(1)} %get-tuple-element.21), channel_id=1, source_target_pairs={{0,8},{4,12},{8,16},{12,20},{16,24},{20,28},{24,0},{28,4},{1,9},{5... | collective-permute-start | bytes 786440 | tf_op jit(solution)/shard_map/ppermute | solution.py:41
  37.2 15.9 %collective-permute-start.15 = (bf16[2,128,512]{2,1,0:T(8,128)(2,1)S(1)}, bf16[2,128,512]{2,1,0:T(8,128)(2,1)S(1)}, u32[]{:S(2)}, u32[]{:S(2)}) collective-permute-start(bf16[2,128,512]{2,1,0:T(8,128)(2,1)S(1)} %get-tuple-element.22), channel_id=1, source_target_pairs={{0,24},{4,28},{8,0},{12,4},{16,8},{20,12},{24,16},{28,20},{1,25},{... | collective-permute-start | bytes 786440 | tf_op jit(solution)/shard_map/ppermute | solution.py:41
  40.3 14.8 %collective-permute-start.1 = (bf16[2,128,512]{2,1,0:T(8,128)(2,1)S(1)}, bf16[2,128,512]{2,1,0:T(8,128)(2,1)S(1)}, u32[]{:S(2)}, u32[]{:S(2)}) collective-permute-start(bf16[2,128,512]{2,1,0:T(8,128)(2,1)S(1)} %get-tuple-element.15), channel_id=1, source_target_pairs={{0,16},{4,20},{8,24},{12,28},{16,0},{20,4},{24,8},{28,12},{1,17},{... | collective-permute-start | bytes 786440 | tf_op jit(solution)/shard_map/ppermute | solution.py:41
  42.9 12.5 %collective-permute-start.11 = (bf16[2,64,512]{2,1,0:T(8,128)(2,1)S(1)}, bf16[2,64,512]{2,1,0:T(8,128)(2,1)S(1)}, u32[]{:S(2)}, u32[]{:S(2)}) collective-permute-start(bf16[2,64,512]{2,1,0:T(8,128)(2,1)S(1)} %slice.18), channel_id=1, source_target_pairs={{0,8},{4,12},{8,16},{12,20},{16,24},{20,28},{24,0},{28,4},{1,9},{5... | collective-permute-start | bytes 393224 | tf_op jit(solution)/shard_map/ppermute | solution.py:41
  43.1 12.6 %collective-permute-start.13 = (bf16[2,64,512]{2,1,0:T(8,128)(2,1)S(1)}, bf16[2,64,512]{2,1,0:T(8,128)(2,1)S(1)}, u32[]{:S(2)}, u32[]{:S(2)}) collective-permute-start(bf16[2,64,512]{2,1,0:T(8,128)(2,1)S(1)} %slice.19), channel_id=1, source_target_pairs={{0,24},{4,28},{8,0},{12,4},{16,8},{20,12},{24,16},{28,20},{1,25},{... | collective-permute-start | bytes 393224 | tf_op jit(solution)/shard_map/ppermute | solution.py:41
  56.6 2.0 %collective-permute-start.16 = (bf16[4,2,2,32,512]{4,3,2,1,0:T(8,128)(2,1)S(1)}, bf16[4,2,2,32,512]{4,3,2,1,0:T(8,128)(2,1)S(1)}, u32[]{:S(2)}, u32[]{:S(2)}) collective-permute-start(bf16[4,2,2,32,512]{4,3,2,1,0:T(8,128)(2,1)S(1)} %get-tuple-element.24), channel_id=1, source_target_pairs={{0,4},{4,0},{8,12},{12,8},{16,20},{20,16},{24,28},{28,24},{1,5},{5... | collective-permute-start | bytes 1572872 | tf_op jit(solution)/shard_map/ppermute | solution.py:37
  58.8 6.9 %collective-permute-start.20 = (bf16[2,32,512]{2,1,0:T(8,128)(2,1)S(1)}, bf16[2,32,512]{2,1,0:T(8,128)(2,1)S(1)}, u32[]{:S(2)}, u32[]{:S(2)}) collective-permute-start(bf16[2,32,512]{2,1,0:T(8,128)(2,1)S(1)} %get-tuple-element.29), channel_id=1, source_target_pairs={{0,64},{32,96},{64,0},{96,32},{128,192},{160,224},{192,128},{224,1... | collective-permute-start | bytes 196616 | tf_op jit(solution)/shard_map/ppermute | solution.py:45
  60.3 6.3 %collective-permute-start.21 = (bf16[2,32,512]{2,1,0:T(8,128)(2,1)S(1)}, bf16[2,32,512]{2,1,0:T(8,128)(2,1)S(1)}, u32[]{:S(2)}, u32[]{:S(2)}) collective-permute-start(bf16[2,32,512]{2,1,0:T(8,128)(2,1)S(1)} %get-tuple-element.28), channel_id=1, source_target_pairs={{0,32},{32,64},{64,96},{96,0},{128,160},{160,192},{192,224},{224,1... | collective-permute-start | bytes 196616 | tf_op jit(solution)/shard_map/ppermute | solution.py:45
  62.4 6.5 %collective-permute-start.22 = (bf16[2,32,512]{2,1,0:T(8,128)(2,1)S(1)}, bf16[2,32,512]{2,1,0:T(8,128)(2,1)S(1)}, u32[]{:S(2)}, u32[]{:S(2)}) collective-permute-start(bf16[2,32,512]{2,1,0:T(8,128)(2,1)S(1)} %get-tuple-element.27), channel_id=1, source_target_pairs={{0,96},{32,0},{64,32},{96,64},{128,224},{160,128},{192,160},{224,1... | collective-permute-start | bytes 196616 | tf_op jit(solution)/shard_map/ppermute | solution.py:45
  62.4 11.9 %collective-permute-start.17 = (bf16[2,32,512]{2,1,0:T(8,128)(2,1)S(1)}, bf16[2,32,512]{2,1,0:T(8,128)(2,1)S(1)}, u32[]{:S(2)}, u32[]{:S(2)}) collective-permute-start(bf16[2,32,512]{2,1,0:T(8,128)(2,1)S(1)} %get-tuple-element.32), channel_id=1, source_target_pairs={{0,64},{32,96},{64,0},{96,32},{128,192},{160,224},{192,128},{224,1... | collective-permute-start | bytes 196616 | tf_op jit(solution)/shard_map/ppermute | solution.py:45
  64.5 9.8 %collective-permute-start.18 = (bf16[2,32,512]{2,1,0:T(8,128)(2,1)S(1)}, bf16[2,32,512]{2,1,0:T(8,128)(2,1)S(1)}, u32[]{:S(2)}, u32[]{:S(2)}) collective-permute-start(bf16[2,32,512]{2,1,0:T(8,128)(2,1)S(1)} %get-tuple-element.31), channel_id=1, source_target_pairs={{0,32},{32,64},{64,96},{96,0},{128,160},{160,192},{192,224},{224,1... | collective-permute-start | bytes 196616 | tf_op jit(solution)/shard_map/ppermute | solution.py:45
  65.7 8.6 %collective-permute-start.19 = (bf16[2,32,512]{2,1,0:T(8,128)(2,1)S(1)}, bf16[2,32,512]{2,1,0:T(8,128)(2,1)S(1)}, u32[]{:S(2)}, u32[]{:S(2)}) collective-permute-start(bf16[2,32,512]{2,1,0:T(8,128)(2,1)S(1)} %get-tuple-element.30), channel_id=1, source_target_pairs={{0,96},{32,0},{64,32},{96,64},{128,224},{160,128},{192,160},{224,1... | collective-permute-start | bytes 196616 | tf_op jit(solution)/shard_map/ppermute | solution.py:45
  68.9 8.3 %collective-permute-start.23 = (bf16[2,32,512]{2,1,0:T(8,128)(2,1)S(1)}, bf16[2,32,512]{2,1,0:T(8,128)(2,1)S(1)}, u32[]{:S(2)}, u32[]{:S(2)}) collective-permute-start(bf16[2,32,512]{2,1,0:T(8,128)(2,1)S(1)} %join.1), channel_id=1, source_target_pairs={{0,128},{32,160},{64,192},{96,224},{128,0},{160,32},{192,64},{224,... | collective-permute-start | bytes 196616 | tf_op jit(solution)/shard_map/ppermute | solution.py:49
  (5 other events, 24.4 us)

commit v2 on v1

--- a/solution.py
+++ b/solution.py
@@ -131,12 +131,12 @@
     return lax.axis_index("fine") & 1
 
 
-def pack_kernel(own_ref, other_ref, *out_refs):
+def pack_kernel(shifts, own_ref, other_ref, *out_refs):
     fine = lax.axis_index("fine")
     k = fine & 1
     rows = own_ref.shape[2]
     low = lax.broadcasted_iota(jnp.int32, (rows, 128), 1) < 64
-    for d, out in enumerate(out_refs):
+    for d, out in zip(shifts, out_refs):
         y = ((fine >> 1) + d) & 3
         even = (y & 1) == 0
         base = pl.multiple_of((y >> 1) * 128, 128)
@@ -149,16 +149,16 @@
                 out[0, at, p * 128 : (p + 1) * 128] = jnp.where(low, jnp.where(even, a, c), jnp.where(even, c, b)).astype(BF16)
 
 
-def pack(own, other):
+def pack(shifts, own, other):
     _, i, rows, m = own.shape
     shape = jax.ShapeDtypeStruct((2, 2 * rows, m // 4), BF16)
     window = pl.BlockSpec((1, 1, rows, m), lambda g: (core(), g, 0, 0))
     return pl.pallas_call(
-        pack_kernel,
+        lambda *refs: pack_kernel(shifts, *refs),
         grid=(i,),
         in_specs=[window, window],
-        out_specs=[pl.BlockSpec((1,) + shape.shape[1:], lambda g: (g, 0, 0))] * 4,
-        out_shape=[shape] * 4,
+        out_specs=[pl.BlockSpec((1,) + shape.shape[1:], lambda g: (g, 0, 0))] * len(shifts),
+        out_shape=[shape] * len(shifts),
         name="pack",
         compiler_params=PARAMS,
     )(own, other)
@@ -451,7 +451,9 @@
     ph_own = jnp.transpose(phase1, (1, 0, 2))
     ph_other = swap_cores(ph_own)
     band = bands(replica)
-    u2_parts = pack(upsample2, u2_other)
+    (u2_far,) = pack((2,), upsample2, u2_other)
+    u2_own, u2_after, u2_before = pack((0, 1, 3), upsample2, u2_other)
+    u2_parts = [u2_own, u2_after, u2_far, u2_before]
     samples = prep(echoes, expo)
     u2_parts = [u2_parts[0]] + [shift_chips(u2_parts[d], d) for d in (1, 2, 3)]
 

time: 78.1 us -> 78.1 us (level)
  no operation moved by 1% of the time
where the time goes in v2:
time: 78.1 us; the launch traced here: 77.9 us
  starting transfers between devices  36.9 us (47%)
  waiting for transfers between devices  20 us (26%)
  Pallas kernels  15.3 us (20%)
  local copies, waits for them, and re-layouts  4.93 us (6%)
    ppermute x10, starting transfers between devices, shift_chips(): lax.ppermute(x, 'fine', [(y * 2 + k, (y + d) % 4 * 2 + k) for y in range(...  17.2 us
    ppermute x10, waiting for transfers between devices, shift_chips(): lax.ppermute(x, 'fine', [(y * 2 + k, (y + d) % 4 * 2 + k) for y in range(...  11.7 us
    ppermute x6, starting transfers between devices, shift_x(): lax.ppermute(x, 'coarse', [(z * 4 + i, z * 4 + (i + d) % 4) for z in rang...  7.76 us
    pallas_call x4, Pallas kernels, level_part(): pl.pallas_call(lambda *refs: level_kernel(d, *refs), in_specs=[WHOLE] * 5...  6.07 us
    ppermute x1, starting transfers between devices, program(): odd = lax.ppermute(odd, 'swath', [(0, 0), (1, 2), (2, 1), (3, 3)])  5.62 us
    ppermute x1, starting transfers between devices, swap_z(): return lax.ppermute(x, 'coarse', [(i, i ^ 4) for i in range(8)])  5.35 us
    ppermute x1, waiting for transfers between devices, swap_z(): return lax.ppermute(x, 'coarse', [(i, i ^ 4) for i in range(8)])  2.89 us
    dynamic_slice x1, local copies, waits for them, and re-layouts, pick(): return lax.dynamic_index_in_dim(x, i, axis, keepdims=False)  2.39 us
  transfers between devices with their start and end apart: 24, of which 12 were waited for; matrix products, arithmetic and copies ran while one was open for 4% of the time, Pallas kernels for 18%

profile of v2, /device:TPU:38, one launch (start us, length us, event | category | flops | bytes accessed | tf_op | source)
XLA Modules:
  0.0 77.9 jit_solution(2566196202108389187)
XLA Ops:
  0.0 2.1 %copy.13 = bf16[512,4,512]{2,0,1:T(8,128)(2,1)S(1)} copy(bf16[512,4,512]{2,1,0:T(4,128)(2,1)} %param.13) | data formatting | bytes 4194304 | tf_op args[5]
  3.6 5.6 %collective-permute-start.5 = (bf16[4,64,128]{2,1,0:T(8,128)(2,1)S(1)}, bf16[4,64,128]{2,1,0:T(8,128)(2,1)S(1)}, u32[]{:S(2)}, u32[]{:S(2)}) collective-permute-start(bf16[4,64,128]{2,1,0:T(8,128)(2,1)S(1)} %get-tuple-element.17), channel_id=1, source_target_pairs={{0,0},{1,2},{2,1},{3,3},{4,4},{5,6},{6,5},{7,7},{8,8},{9,10},{10,9... | collective-permute-start | bytes 196616 | tf_op jit(solution)/shard_map/ppermute | solution.py:450
  13.1 1.7 %weights.1 = (bf16[4,2,512,128]{3,2,1,0:T(8,128)(2,1)S(1)}, bf16[2,512,512]{2,1,0:T(8,128)(2,1)S(1)}) custom-call(bf16[2,4,64,512]{3,2,1,0:T(8,128)(2,1)} %u_own.1, bf16[2,4,64,512]{3,2,1,0:T(8,128)(2,1)} %collective-permute-done.2.u_other, bf16[4,512,512]{2,1,0:T(8,128)(2,1)} %collective-permute-done.3.ph_other), custom_call_target="tpu_custom_call" | custom-call | tf_op jit(solution)/shard_map/weights/pallas_call | solution.py:183
  14.8 1.5 %level.5 = bf16[2,128,512]{2,1,0:T(8,128)(2,1)S(1)} custom-call(bf16[4,2,512,128]{3,2,1,0:T(8,128)(2,1)S(1)} %get-tuple-element.14.refs_0_, bf16[4,512,512]{2,1,0:T(8,128)(2,1)S(1)} %bitcast.23, bf16[2,512,512]{2,1,0:T(8,128)(2,1)S(1)} %get-tuple-element.15.refs_2_, bf16[4,2,64,512]{3,2,1,0:T(8,128)(2,1)S(1)} %beams.1.refs_3_, ...), custom_call_target="tpu_custom_call" | custom-call | tf_op jit(solution)/shard_map/level/pallas_call | solution.py:299
  16.4 3.3 %collective-permute-start.7 = (bf16[2,128,512]{2,1,0:T(8,128)(2,1)S(1)}, bf16[2,128,512]{2,1,0:T(8,128)(2,1)S(1)}, u32[]{:S(2)}, u32[]{:S(2)}) collective-permute-start(bf16[2,128,512]{2,1,0:T(8,128)(2,1)S(1)} %level.5), channel_id=1, source_target_pairs={{0,16},{4,20},{8,24},{12,28},{16,0},{20,4},{24,8},{28,12},{1,17},{... | collective-permute-start | bytes 786440 | tf_op jit(solution)/shard_map/ppermute | solution.py:41
  19.7 1.5 %level.6 = bf16[2,128,512]{2,1,0:T(8,128)(2,1)S(1)} custom-call(bf16[4,2,512,128]{3,2,1,0:T(8,128)(2,1)S(1)} %get-tuple-element.14.refs_0_, bf16[4,512,512]{2,1,0:T(8,128)(2,1)S(1)} %bitcast.24, bf16[2,512,512]{2,1,0:T(8,128)(2,1)S(1)} %get-tuple-element.15.refs_2_, bf16[4,2,64,512]{3,2,1,0:T(8,128)(2,1)S(1)} %beams.1.refs_3_, ...), custom_call_target="tpu_custom_call" | custom-call | tf_op jit(solution)/shard_map/level/pallas_call | solution.py:299
  21.9 1.5 %level.7 = bf16[2,128,512]{2,1,0:T(8,128)(2,1)S(1)} custom-call(bf16[4,2,512,128]{3,2,1,0:T(8,128)(2,1)S(1)} %get-tuple-element.14.refs_0_, bf16[4,512,512]{2,1,0:T(8,128)(2,1)S(1)} %bitcast.25, bf16[2,512,512]{2,1,0:T(8,128)(2,1)S(1)} %get-tuple-element.15.refs_2_, bf16[4,2,64,512]{3,2,1,0:T(8,128)(2,1)S(1)} %beams.1.refs_3_, ...), custom_call_target="tpu_custom_call" | custom-call | tf_op jit(solution)/shard_map/level/pallas_call | solution.py:299
  23.5 2.6 %collective-permute-start.9 = (bf16[2,128,512]{2,1,0:T(8,128)(2,1)S(1)}, bf16[2,128,512]{2,1,0:T(8,128)(2,1)S(1)}, u32[]{:S(2)}, u32[]{:S(2)}) collective-permute-start(bf16[2,128,512]{2,1,0:T(8,128)(2,1)S(1)} %level.7), channel_id=1, source_target_pairs={{0,24},{4,28},{8,0},{12,4},{16,8},{20,12},{24,16},{28,20},{1,25},{... | collective-permute-start | bytes 786440 | tf_op jit(solution)/shard_map/ppermute | solution.py:41
  26.1 1.5 %level.4 = f32[2,128,512]{2,1,0:T(8,128)S(1)} custom-call(bf16[4,2,512,128]{3,2,1,0:T(8,128)(2,1)S(1)} %get-tuple-element.14.refs_0_, bf16[4,512,512]{2,1,0:T(8,128)(2,1)S(1)} %bitcast.26, bf16[2,512,512]{2,1,0:T(8,128)(2,1)S(1)} %get-tuple-element.15.refs_2_, bf16[4,2,64,512]{3,2,1,0:T(8,128)(2,1)S(1)} %beams.1.refs_3_, ...), custom_call_target="tpu_custom_call" | custom-call | tf_op jit(solution)/shard_map/level/pallas_call | solution.py:299
  27.6 4.3 %collective-permute-done.8 = bf16[2,128,512]{2,1,0:T(8,128)(2,1)S(1)} collective-permute-done((bf16[2,128,512]{2,1,0:T(8,128)(2,1)S(1)}, bf16[2,128,512]{2,1,0:T(8,128)(2,1)S(1)}, u32[]{:S(2)}, u32[]{:S(2)}) %collective-permute-start.8) | collective-permute-done | bytes 262176 | tf_op jit(solution)/shard_map/ppermute | solution.py:41
  32.4 1.5 %collective-permute-start.10 = (bf16[2,128,512]{2,1,0:T(8,128)(2,1)S(1)}, bf16[2,128,512]{2,1,0:T(8,128)(2,1)S(1)}, u32[]{:S(2)}, u32[]{:S(2)}) collective-permute-start(bf16[2,128,512]{2,1,0:T(8,128)(2,1)S(1)} %add_convert_fusion.1.refs_3_), channel_id=1, source_target_pairs={{0,8},{4,12},{8,16},{12,20},{16,24},{20,28},{24,0},{28,4},{1,9},{5... | collective-permute-start | bytes 786440 | tf_op jit(solution)/shard_map/ppermute | solution.py:41
  33.9 1.9 %collective-permute-start.12 = (bf16[2,128,512]{2,1,0:T(8,128)(2,1)S(1)}, bf16[2,128,512]{2,1,0:T(8,128)(2,1)S(1)}, u32[]{:S(2)}, u32[]{:S(2)}) collective-permute-start(bf16[2,128,512]{2,1,0:T(8,128)(2,1)S(1)} %add_convert_fusion.1.refs_3_), channel_id=1, source_target_pairs={{0,24},{4,28},{8,0},{12,4},{16,8},{20,12},{24,16},{28,20},{1,25},{... | collective-permute-start | bytes 786440 | tf_op jit(solution)/shard_map/ppermute | solution.py:41
  36.8 3.1 %collective-permute-start.15 = (bf16[2,128,512]{2,1,0:T(8,128)(2,1)S(1)}, bf16[2,128,512]{2,1,0:T(8,128)(2,1)S(1)}, u32[]{:S(2)}, u32[]{:S(2)}) collective-permute-start(bf16[2,128,512]{2,1,0:T(8,128)(2,1)S(1)} %get-tuple-element.20), channel_id=1, source_target_pairs={{0,24},{4,28},{8,0},{12,4},{16,8},{20,12},{24,16},{28,20},{1,25},{... | collective-permute-start | bytes 786440 | tf_op jit(solution)/shard_map/ppermute | solution.py:41
  40.7 2.2 %collective-permute-done.10.refs_4_ = bf16[2,128,512]{2,1,0:T(8,128)(2,1)S(1)} collective-permute-done((bf16[2,128,512]{2,1,0:T(8,128)(2,1)S(1)}, bf16[2,128,512]{2,1,0:T(8,128)(2,1)S(1)}, u32[]{:S(2)}, u32[]{:S(2)}) %collective-permute-start.10) | collective-permute-done | bytes 262176 | tf_op jit(solution)/shard_map/ppermute | solution.py:41
  43.1 3.1 %collective-permute-start.13 = (bf16[2,64,512]{2,1,0:T(8,128)(2,1)S(1)}, bf16[2,64,512]{2,1,0:T(8,128)(2,1)S(1)}, u32[]{:S(2)}, u32[]{:S(2)}) collective-permute-start(bf16[2,64,512]{2,1,0:T(8,128)(2,1)S(1)} %slice.19), channel_id=1, source_target_pairs={{0,24},{4,28},{8,0},{12,4},{16,8},{20,12},{24,16},{28,20},{1,25},{... | collective-permute-start | bytes 393224 | tf_op jit(solution)/shard_map/ppermute | solution.py:41
  46.3 2.4 %constant_dynamic-slice_fusion = bf16[8,1,64,1,512]{4,3,2,1,0:T(2,128)(2,1)S(1)} fusion(bf16[8,4,64,2,512]{4,3,2,1,0:T(2,128)(2,1)} %bitcast.30, s32[]{:T(128)S(6)} %select_n.99, s32[]{:T(128)S(6)} %select_n.102), kind=kLoop, calls=%fused_computation.12 | loop fusion | bytes 1048584 | tf_op jit(solution)/shard_map/jit(dynamic_index_in_dim)/dynamic_slice | solution.py:53
  49.8 2.6 %collective-permute-done.14.refs_1_ = bf16[2,128,512]{2,1,0:T(8,128)(2,1)S(1)} collective-permute-done((bf16[2,128,512]{2,1,0:T(8,128)(2,1)S(1)}, bf16[2,128,512]{2,1,0:T(8,128)(2,1)S(1)}, u32[]{:S(2)}, u32[]{:S(2)}) %collective-permute-start.14) | collective-permute-done | bytes 262176 | tf_op jit(solution)/shard_map/ppermute | solution.py:41
  56.8 1.8 %collective-permute-done.16 = bf16[4,2,2,32,512]{4,3,2,1,0:T(8,128)(2,1)S(1)} collective-permute-done((bf16[4,2,2,32,512]{4,3,2,1,0:T(8,128)(2,1)S(1)}, bf16[4,2,2,32,512]{4,3,2,1,0:T(8,128)(2,1)S(1)}, u32[]{:S(2)}, u32[]{:S(2)}) %collective-permute-start.16) | collective-permute-done | bytes 524320 | tf_op jit(solution)/shard_map/ppermute | solution.py:37
  58.8 1.5 %collective-permute-start.20 = (bf16[2,32,512]{2,1,0:T(8,128)(2,1)S(1)}, bf16[2,32,512]{2,1,0:T(8,128)(2,1)S(1)}, u32[]{:S(2)}, u32[]{:S(2)}) collective-permute-start(bf16[2,32,512]{2,1,0:T(8,128)(2,1)S(1)} %get-tuple-element.27), channel_id=1, source_target_pairs={{0,64},{32,96},{64,0},{96,32},{128,192},{160,224},{192,128},{224,1... | collective-permute-start | bytes 196616 | tf_op jit(solution)/shard_map/ppermute | solution.py:45
  60.3 2.1 %collective-permute-start.21 = (bf16[2,32,512]{2,1,0:T(8,128)(2,1)S(1)}, bf16[2,32,512]{2,1,0:T(8,128)(2,1)S(1)}, u32[]{:S(2)}, u32[]{:S(2)}) collective-permute-start(bf16[2,32,512]{2,1,0:T(8,128)(2,1)S(1)} %get-tuple-element.26), channel_id=1, source_target_pairs={{0,32},{32,64},{64,96},{96,0},{128,160},{160,192},{192,224},{224,1... | collective-permute-start | bytes 196616 | tf_op jit(solution)/shard_map/ppermute | solution.py:45
  62.4 2.1 %collective-permute-start.17 = (bf16[2,32,512]{2,1,0:T(8,128)(2,1)S(1)}, bf16[2,32,512]{2,1,0:T(8,128)(2,1)S(1)}, u32[]{:S(2)}, u32[]{:S(2)}) collective-permute-start(bf16[2,32,512]{2,1,0:T(8,128)(2,1)S(1)} %get-tuple-element.30), channel_id=1, source_target_pairs={{0,64},{32,96},{64,0},{96,32},{128,192},{160,224},{192,128},{224,1... | collective-permute-start | bytes 196616 | tf_op jit(solution)/shard_map/ppermute | solution.py:45
  66.6 2.3 %collective-permute-done.22.refs_3_ = bf16[2,32,512]{2,1,0:T(8,128)(2,1)S(1)} collective-permute-done((bf16[2,32,512]{2,1,0:T(8,128)(2,1)S(1)}, bf16[2,32,512]{2,1,0:T(8,128)(2,1)S(1)}, u32[]{:S(2)}, u32[]{:S(2)}) %collective-permute-start.22) | collective-permute-done | bytes 65568 | tf_op jit(solution)/shard_map/ppermute | solution.py:45
  68.9 5.4 %collective-permute-start.23 = (bf16[2,32,512]{2,1,0:T(8,128)(2,1)S(1)}, bf16[2,32,512]{2,1,0:T(8,128)(2,1)S(1)}, u32[]{:S(2)}, u32[]{:S(2)}) collective-permute-start(bf16[2,32,512]{2,1,0:T(8,128)(2,1)S(1)} %join.1), channel_id=1, source_target_pairs={{0,128},{32,160},{64,192},{96,224},{128,0},{160,32},{192,64},{224,... | collective-permute-start | bytes 196616 | tf_op jit(solution)/shard_map/ppermute | solution.py:49
  74.3 2.9 %collective-permute-done.23.refs_4_ = bf16[2,32,512]{2,1,0:T(8,128)(2,1)S(1)} collective-permute-done((bf16[2,32,512]{2,1,0:T(8,128)(2,1)S(1)}, bf16[2,32,512]{2,1,0:T(8,128)(2,1)S(1)}, u32[]{:S(2)}, u32[]{:S(2)}) %collective-permute-start.23) | collective-permute-done | bytes 65568 | tf_op jit(solution)/shard_map/ppermute | solution.py:49
  (65 shorter events, 17.1 us)
Async XLA Ops:
  2.1 11.0 %collective-permute-start.3 = (bf16[4,512,512]{2,1,0:T(8,128)(2,1)S(1)}, bf16[4,512,512]{2,1,0:T(8,128)(2,1)}, u32[]{:S(2)}, u32[]{:S(2)}) collective-permute-start(bf16[4,512,512]{2,1,0:T(8,128)(2,1)S(1)} %bitcast.22), channel_id=1, source_target_pairs={{0,4},{4,0},{8,12},{12,8},{16,20},{20,16},{24,28},{28,24},{1,5},{5... | collective-permute-start | bytes 6291464 | tf_op jit(solution)/shard_map/ppermute | solution.py:37
  3.5 6.8 %collective-permute-start.4 = (bf16[4,64,128]{2,1,0:T(8,128)(2,1)}, bf16[4,64,128]{2,1,0:T(8,128)(2,1)S(1)}, u32[]{:S(2)}, u32[]{:S(2)}) collective-permute-start(bf16[4,64,128]{2,1,0:T(8,128)(2,1)} %get-tuple-element.16), channel_id=1, source_target_pairs={{0,1},{1,0},{2,3},{3,2},{4,5},{5,4},{6,7},{7,6},{8,9},{9,8},{10,11... | collective-permute-start | bytes 196616 | tf_op jit(solution)/shard_map/ppermute | solution.py:449
  3.6 8.1 %collective-permute-start.5 = (bf16[4,64,128]{2,1,0:T(8,128)(2,1)S(1)}, bf16[4,64,128]{2,1,0:T(8,128)(2,1)S(1)}, u32[]{:S(2)}, u32[]{:S(2)}) collective-permute-start(bf16[4,64,128]{2,1,0:T(8,128)(2,1)S(1)} %get-tuple-element.17), channel_id=1, source_target_pairs={{0,0},{1,2},{2,1},{3,3},{4,4},{5,6},{6,5},{7,7},{8,8},{9,10},{10,9... | collective-permute-start | bytes 196616 | tf_op jit(solution)/shard_map/ppermute | solution.py:450
  9.3 3.8 %collective-permute-start.2 = (bf16[2,4,64,512]{3,2,1,0:T(8,128)(2,1)}, bf16[2,4,64,512]{3,2,1,0:T(8,128)(2,1)}, u32[]{:S(2)}, u32[]{:S(2)}) collective-permute-start(bf16[2,4,64,512]{3,2,1,0:T(8,128)(2,1)} %u_own.1), channel_id=1, source_target_pairs={{0,4},{4,0},{8,12},{12,8},{16,20},{20,16},{24,28},{28,24},{1,5},{5... | collective-permute-start | bytes 1572872 | tf_op jit(solution)/shard_map/ppermute | solution.py:37
  12.5 2.3 %collective-permute-start.6 = (bf16[4,2,64,512]{3,2,1,0:T(8,128)(2,1)S(1)}, bf16[4,2,64,512]{3,2,1,0:T(8,128)(2,1)S(1)}, u32[]{:S(2)}, u32[]{:S(2)}) collective-permute-start(bf16[4,2,64,512]{3,2,1,0:T(8,128)(2,1)S(1)} %beams.1.refs_3_), channel_id=1, source_target_pairs={{0,4},{4,0},{8,12},{12,8},{16,20},{20,16},{24,28},{28,24},{1,5},{5... | collective-permute-start | bytes 1572872 | tf_op jit(solution)/shard_map/ppermute | solution.py:37
  12.6 23.1 %collective-permute-start = (bf16[2,2,64,2048]{3,2,1,0:T(8,128)(2,1)S(1)}, bf16[2,2,64,2048]{3,2,1,0:T(8,128)(2,1)S(1)}, u32[]{:S(2)}, u32[]{:S(2)}) collective-permute-start(bf16[2,2,64,2048]{3,2,1,0:T(8,128)(2,1)S(1)} %copy-done.1), channel_id=1, source_target_pairs={{0,4},{4,0},{8,12},{12,8},{16,20},{20,16},{24,28},{28,24},{1,5},{5... | collective-permute-start | bytes 3145736 | tf_op jit(solution)/shard_map/ppermute | solution.py:37
  16.4 11.3 %collective-permute-start.7 = (bf16[2,128,512]{2,1,0:T(8,128)(2,1)S(1)}, bf16[2,128,512]{2,1,0:T(8,128)(2,1)S(1)}, u32[]{:S(2)}, u32[]{:S(2)}) collective-permute-start(bf16[2,128,512]{2,1,0:T(8,128)(2,1)S(1)} %level.5), channel_id=1, source_target_pairs={{0,16},{4,20},{8,24},{12,28},{16,0},{20,4},{24,8},{28,12},{1,17},{... | collective-permute-start | bytes 786440 | tf_op jit(solution)/shard_map/ppermute | solution.py:41
  21.2 10.7 %collective-permute-start.8 = (bf16[2,128,512]{2,1,0:T(8,128)(2,1)S(1)}, bf16[2,128,512]{2,1,0:T(8,128)(2,1)S(1)}, u32[]{:S(2)}, u32[]{:S(2)}) collective-permute-start(bf16[2,128,512]{2,1,0:T(8,128)(2,1)S(1)} %level.6), channel_id=1, source_target_pairs={{0,8},{4,12},{8,16},{12,20},{16,24},{20,28},{24,0},{28,4},{1,9},{5... | collective-permute-start | bytes 786440 | tf_op jit(solution)/shard_map/ppermute | solution.py:41
  23.5 8.8 %collective-permute-start.9 = (bf16[2,128,512]{2,1,0:T(8,128)(2,1)S(1)}, bf16[2,128,512]{2,1,0:T(8,128)(2,1)S(1)}, u32[]{:S(2)}, u32[]{:S(2)}) collective-permute-start(bf16[2,128,512]{2,1,0:T(8,128)(2,1)S(1)} %level.7), channel_id=1, source_target_pairs={{0,24},{4,28},{8,0},{12,4},{16,8},{20,12},{24,16},{28,20},{1,25},{... | collective-permute-start | bytes 786440 | tf_op jit(solution)/shard_map/ppermute | solution.py:41
  32.4 10.5 %collective-permute-start.10 = (bf16[2,128,512]{2,1,0:T(8,128)(2,1)S(1)}, bf16[2,128,512]{2,1,0:T(8,128)(2,1)S(1)}, u32[]{:S(2)}, u32[]{:S(2)}) collective-permute-start(bf16[2,128,512]{2,1,0:T(8,128)(2,1)S(1)} %add_convert_fusion.1.refs_3_), channel_id=1, source_target_pairs={{0,8},{4,12},{8,16},{12,20},{16,24},{20,28},{24,0},{28,4},{1,9},{5... | collective-permute-start | bytes 786440 | tf_op jit(solution)/shard_map/ppermute | solution.py:41
  33.9 9.3 %collective-permute-start.12 = (bf16[2,128,512]{2,1,0:T(8,128)(2,1)S(1)}, bf16[2,128,512]{2,1,0:T(8,128)(2,1)S(1)}, u32[]{:S(2)}, u32[]{:S(2)}) collective-permute-start(bf16[2,128,512]{2,1,0:T(8,128)(2,1)S(1)} %add_convert_fusion.1.refs_3_), channel_id=1, source_target_pairs={{0,24},{4,28},{8,0},{12,4},{16,8},{20,12},{24,16},{28,20},{1,25},{... | collective-permute-start | bytes 786440 | tf_op jit(solution)/shard_map/ppermute | solution.py:41
  36.5 15.9 %collective-permute-start.14 = (bf16[2,128,512]{2,1,0:T(8,128)(2,1)S(1)}, bf16[2,128,512]{2,1,0:T(8,128)(2,1)S(1)}, u32[]{:S(2)}, u32[]{:S(2)}) collective-permute-start(bf16[2,128,512]{2,1,0:T(8,128)(2,1)S(1)} %get-tuple-element.19), channel_id=1, source_target_pairs={{0,8},{4,12},{8,16},{12,20},{16,24},{20,28},{24,0},{28,4},{1,9},{5... | collective-permute-start | bytes 786440 | tf_op jit(solution)/shard_map/ppermute | solution.py:41
  36.8 16.3 %collective-permute-start.15 = (bf16[2,128,512]{2,1,0:T(8,128)(2,1)S(1)}, bf16[2,128,512]{2,1,0:T(8,128)(2,1)S(1)}, u32[]{:S(2)}, u32[]{:S(2)}) collective-permute-start(bf16[2,128,512]{2,1,0:T(8,128)(2,1)S(1)} %get-tuple-element.20), channel_id=1, source_target_pairs={{0,24},{4,28},{8,0},{12,4},{16,8},{20,12},{24,16},{28,20},{1,25},{... | collective-permute-start | bytes 786440 | tf_op jit(solution)/shard_map/ppermute | solution.py:41
  40.2 14.9 %collective-permute-start.1 = (bf16[2,128,512]{2,1,0:T(8,128)(2,1)S(1)}, bf16[2,128,512]{2,1,0:T(8,128)(2,1)S(1)}, u32[]{:S(2)}, u32[]{:S(2)}) collective-permute-start(bf16[2,128,512]{2,1,0:T(8,128)(2,1)S(1)} %pack.2), channel_id=1, source_target_pairs={{0,16},{4,20},{8,24},{12,28},{16,0},{20,4},{24,8},{28,12},{1,17},{... | collective-permute-start | bytes 786440 | tf_op jit(solution)/shard_map/ppermute | solution.py:41
  42.9 12.5 %collective-permute-start.11 = (bf16[2,64,512]{2,1,0:T(8,128)(2,1)S(1)}, bf16[2,64,512]{2,1,0:T(8,128)(2,1)S(1)}, u32[]{:S(2)}, u32[]{:S(2)}) collective-permute-start(bf16[2,64,512]{2,1,0:T(8,128)(2,1)S(1)} %slice.18), channel_id=1, source_target_pairs={{0,8},{4,12},{8,16},{12,20},{16,24},{20,28},{24,0},{28,4},{1,9},{5... | collective-permute-start | bytes 393224 | tf_op jit(solution)/shard_map/ppermute | solution.py:41
  43.1 12.6 %collective-permute-start.13 = (bf16[2,64,512]{2,1,0:T(8,128)(2,1)S(1)}, bf16[2,64,512]{2,1,0:T(8,128)(2,1)S(1)}, u32[]{:S(2)}, u32[]{:S(2)}) collective-permute-start(bf16[2,64,512]{2,1,0:T(8,128)(2,1)S(1)} %slice.19), channel_id=1, source_target_pairs={{0,24},{4,28},{8,0},{12,4},{16,8},{20,12},{24,16},{28,20},{1,25},{... | collective-permute-start | bytes 393224 | tf_op jit(solution)/shard_map/ppermute | solution.py:41
  56.6 2.0 %collective-permute-start.16 = (bf16[4,2,2,32,512]{4,3,2,1,0:T(8,128)(2,1)S(1)}, bf16[4,2,2,32,512]{4,3,2,1,0:T(8,128)(2,1)S(1)}, u32[]{:S(2)}, u32[]{:S(2)}) collective-permute-start(bf16[4,2,2,32,512]{4,3,2,1,0:T(8,128)(2,1)S(1)} %get-tuple-element.22), channel_id=1, source_target_pairs={{0,4},{4,0},{8,12},{12,8},{16,20},{20,16},{24,28},{28,24},{1,5},{5... | collective-permute-start | bytes 1572872 | tf_op jit(solution)/shard_map/ppermute | solution.py:37
  58.8 6.9 %collective-permute-start.20 = (bf16[2,32,512]{2,1,0:T(8,128)(2,1)S(1)}, bf16[2,32,512]{2,1,0:T(8,128)(2,1)S(1)}, u32[]{:S(2)}, u32[]{:S(2)}) collective-permute-start(bf16[2,32,512]{2,1,0:T(8,128)(2,1)S(1)} %get-tuple-element.27), channel_id=1, source_target_pairs={{0,64},{32,96},{64,0},{96,32},{128,192},{160,224},{192,128},{224,1... | collective-permute-start | bytes 196616 | tf_op jit(solution)/shard_map/ppermute | solution.py:45
  60.3 6.3 %collective-permute-start.21 = (bf16[2,32,512]{2,1,0:T(8,128)(2,1)S(1)}, bf16[2,32,512]{2,1,0:T(8,128)(2,1)S(1)}, u32[]{:S(2)}, u32[]{:S(2)}) collective-permute-start(bf16[2,32,512]{2,1,0:T(8,128)(2,1)S(1)} %get-tuple-element.26), channel_id=1, source_target_pairs={{0,32},{32,64},{64,96},{96,0},{128,160},{160,192},{192,224},{224,1... | collective-permute-start | bytes 196616 | tf_op jit(solution)/shard_map/ppermute | solution.py:45
  62.4 6.5 %collective-permute-start.22 = (bf16[2,32,512]{2,1,0:T(8,128)(2,1)S(1)}, bf16[2,32,512]{2,1,0:T(8,128)(2,1)S(1)}, u32[]{:S(2)}, u32[]{:S(2)}) collective-permute-start(bf16[2,32,512]{2,1,0:T(8,128)(2,1)S(1)} %get-tuple-element.25), channel_id=1, source_target_pairs={{0,96},{32,0},{64,32},{96,64},{128,224},{160,128},{192,160},{224,1... | collective-permute-start | bytes 196616 | tf_op jit(solution)/shard_map/ppermute | solution.py:45
  62.4 11.9 %collective-permute-start.17 = (bf16[2,32,512]{2,1,0:T(8,128)(2,1)S(1)}, bf16[2,32,512]{2,1,0:T(8,128)(2,1)S(1)}, u32[]{:S(2)}, u32[]{:S(2)}) collective-permute-start(bf16[2,32,512]{2,1,0:T(8,128)(2,1)S(1)} %get-tuple-element.30), channel_id=1, source_target_pairs={{0,64},{32,96},{64,0},{96,32},{128,192},{160,224},{192,128},{224,1... | collective-permute-start | bytes 196616 | tf_op jit(solution)/shard_map/ppermute | solution.py:45
  64.5 9.8 %collective-permute-start.18 = (bf16[2,32,512]{2,1,0:T(8,128)(2,1)S(1)}, bf16[2,32,512]{2,1,0:T(8,128)(2,1)S(1)}, u32[]{:S(2)}, u32[]{:S(2)}) collective-permute-start(bf16[2,32,512]{2,1,0:T(8,128)(2,1)S(1)} %get-tuple-element.29), channel_id=1, source_target_pairs={{0,32},{32,64},{64,96},{96,0},{128,160},{160,192},{192,224},{224,1... | collective-permute-start | bytes 196616 | tf_op jit(solution)/shard_map/ppermute | solution.py:45
  65.7 8.6 %collective-permute-start.19 = (bf16[2,32,512]{2,1,0:T(8,128)(2,1)S(1)}, bf16[2,32,512]{2,1,0:T(8,128)(2,1)S(1)}, u32[]{:S(2)}, u32[]{:S(2)}) collective-permute-start(bf16[2,32,512]{2,1,0:T(8,128)(2,1)S(1)} %get-tuple-element.28), channel_id=1, source_target_pairs={{0,96},{32,0},{64,32},{96,64},{128,224},{160,128},{192,160},{224,1... | collective-permute-start | bytes 196616 | tf_op jit(solution)/shard_map/ppermute | solution.py:45
  68.9 8.3 %collective-permute-start.23 = (bf16[2,32,512]{2,1,0:T(8,128)(2,1)S(1)}, bf16[2,32,512]{2,1,0:T(8,128)(2,1)S(1)}, u32[]{:S(2)}, u32[]{:S(2)}) collective-permute-start(bf16[2,32,512]{2,1,0:T(8,128)(2,1)S(1)} %join.1), channel_id=1, source_target_pairs={{0,128},{32,160},{64,192},{96,224},{128,0},{160,32},{192,64},{224,... | collective-permute-start | bytes 196616 | tf_op jit(solution)/shard_map/ppermute | solution.py:49
  (5 other events, 24.4 us)
